TPU v7x, 32 devices: a whole 2x2x4 slice. The times are simulated.
32 devices in a mesh: groups: 2 (over y), seq: 4 (over z), rows: 2 (over x), cfg: 2 (over core).
Axes of the slice: x: 2, y: 2, z: 4, core: 2. Of those that a mesh axis runs over, the one named last changes fastest.
Arguments:
- hidden: bfloat16 [2, 4096, 5120], P('cfg', ('groups', 'seq', 'rows')), parts along dimension 1, may hold values from -500 to 500
- token_order: int32 [4096], P(('groups', 'seq', 'rows')), parts along dimension 0, may hold values from 0 to 2047, as said below
- noisy_latent: float32 [16, 8, 2048], P(('groups', 'seq'), ('rows', 'cfg')), parts along dimension 0, may hold values from -6 to 6
- head_weight: bfloat16 [5120, 64], replicated, may hold values from -0.078125 to 0.078125
- head_mod: float32 [2, 5120], replicated, may hold values from -2.5 to 2.5
- guidance: float32 [1], replicated, may hold values from 3 to 7
- timestep_index: int32 [1], replicated, may hold values from 0 to 7
- step_table: int32 [9], replicated, may hold values from 0 to 1000, as said below
- vae_mean: float32 [16], replicated, may hold values from -2.5 to 2.5
- vae_std: float32 [16], replicated, may hold values from 1.1 to 3.3
- conv2_weight: float32 [16, 16], replicated, may hold values from -1.5 to 1.5
- conv2_bias: float32 [16], replicated, may hold values from -2.5 to 2.5
- conv1_weight: bfloat16 [27, 16, 384], replicated, may hold values from -0.3125 to 0.3125
- conv1_bias: float32 [384], replicated, may hold values from -2.5 to 2.5
Outputs:
- decoded: bfloat16 [16, 8, 128, 384], P(('groups', 'seq'), ('rows', 'cfg')), parts along dimension 0
There are 2 independent parts, one for each index of `groups`. A program takes and returns all parts, laid end to end along the dimension named above; an argument that names none is the same for every part. Nothing has to cross between parts.
Inputs may be any that keep to these rules, and one draw needn't show every extreme that they name: `token_order`: a permutation of the 2048 cells, cell f * 4 * 64 + i * 64 + j being token column j of token row i of frame f; positions k * 256 to (k + 1) * 256 - 1 with k = s * 2 + r hold exactly the cells of frames s * 2 to (s + 1) * 2 - 1 and token rows r * 2 to (r + 1) * 2 - 1. `step_table`: strictly decreasing from 1000 to 0; consecutive entries differ by 90 or more.
All inputs are finite; a program needn't handle non-finite values.
Results may differ from a plain program's by a relative error of at most 0.0053.
Values may be sent and summed in bfloat16 or wider, within the bound.
No kernel may reach another device: no remote copies, remote signals or barrier semaphores. Data moves between devices by JAX's collectives and lax.ppermute only.
A program may use at most 64 MiB of HBM per device.

v0:
```python
import jax
import jax.numpy as jnp
from jax import lax
from jax.sharding import PartitionSpec as P

FR_DEV = 2
TR_DEV = 2
WT = 64


def padded_2(block, sides, width):
    for axis, dim in sides:
        count = lax.axis_size(axis)
        forward = [(i, i + 1) for i in range(count - 1)]
        backward = [(target, source) for source, target in forward]
        low = lax.ppermute(
            lax.slice_in_dim(block, block.shape[dim] - width, None, axis=dim), axis, forward
        )
        high = lax.ppermute(lax.slice_in_dim(block, 0, width, axis=dim), axis, backward)
        block = jnp.concatenate([low, block, high], axis=dim)
    return block


def shifted(block, axis, distance):
    devices = range(lax.axis_size(axis))
    route = [(i - distance, i) for i in devices if i - distance in devices]
    return lax.ppermute(block, axis, route)


def head_rows(row_block, head_weight, head_mod):
    values = row_block.astype(jnp.float32)
    center = jnp.mean(values, axis=-1, keepdims=True)
    spread = jnp.mean(jnp.square(values - center), axis=-1, keepdims=True)
    normed = (values - center) * lax.rsqrt(spread + 1e-06)
    head_in = (normed * (1.0 + head_mod[1]) + head_mod[0]).astype(jnp.bfloat16)
    return jnp.dot(head_in, head_weight, preferred_element_type=jnp.float32)


def conv_taps(padded, frames, row_count, col_count):
    pieces = []
    for step_time in range(3):
        for step_row in range(3):
            for step_col in range(3):
                pieces.append(
                    padded[
                        step_time : step_time + frames,
                        step_row : step_row + row_count,
                        step_col : step_col + col_count,
                        :,
                    ]
                )
    return jnp.concatenate(pieces, axis=-1)


def per_device(
    hidden,
    token_order,
    noisy_latent,
    head_weight,
    head_mod,
    guidance,
    timestep_index,
    step_table,
    vae_mean,
    vae_std,
    conv2_weight,
    conv2_bias,
    conv1_weight,
    conv1_bias,
):
    token_count = hidden.shape[1]
    patch_width = head_weight.shape[1]
    lat_channels = vae_mean.shape[0]
    out_channels = conv1_weight.shape[2]
    token_rows = TR_DEV * lax.axis_size("rows")
    own_head = head_rows(hidden[0], head_weight, head_mod)
    frame_pos = token_order // (token_rows * WT) % FR_DEV
    row_pos = token_order // WT % TR_DEV
    col_pos = token_order % WT
    local_cell = (frame_pos * TR_DEV + row_pos) * WT + col_pos
    placed = jnp.zeros((token_count, patch_width), jnp.float32).at[local_cell].set(own_head)
    local_block = placed.reshape(FR_DEV, TR_DEV, WT, 2, 2, lat_channels).transpose(0, 1, 3, 2, 4, 5)
    local_block = local_block.reshape(FR_DEV, 2, TR_DEV, 2 * WT * lat_channels)
    gathered = lax.all_gather(local_block[None], "cfg", axis=0, tiled=True)
    half_index = lax.axis_index("cfg")
    conditional = lax.dynamic_index_in_dim(gathered[0], half_index, 1, keepdims=False)
    unconditional = lax.dynamic_index_in_dim(gathered[1], half_index, 1, keepdims=False)
    velocity = unconditional + guidance[0] * (conditional - unconditional)
    step_index = timestep_index[0]
    sigma_now = step_table[step_index].astype(jnp.float32) / 1000.0
    sigma_next = step_table[step_index + 1].astype(jnp.float32) / 1000.0
    stepped = noisy_latent + (sigma_next - sigma_now) * velocity
    channels = stepped.reshape(FR_DEV, TR_DEV, 2 * WT, lat_channels) * vae_std + vae_mean
    mixed_lat = (
        jnp.einsum("fyxc,cd->fyxd", channels, conv2_weight, precision=lax.Precision.HIGHEST)
        + conv2_bias
    )
    latent_in = mixed_lat.astype(jnp.bfloat16).reshape(FR_DEV, TR_DEV, 2 * WT * lat_channels)
    framed = padded_2(latent_in, ((("rows", "cfg"), 1),), 1)
    earlier = shifted(framed, "seq", 1)
    padded = jnp.concatenate([earlier, framed], axis=0).reshape(
        FR_DEV + 2, TR_DEV + 2, 2 * WT, lat_channels
    )
    padded = jnp.pad(padded, ((0, 0), (0, 0), (1, 1), (0, 0)))
    tap_columns = conv_taps(padded, FR_DEV, TR_DEV, 2 * WT).reshape(
        FR_DEV * TR_DEV * 2 * WT, 27 * lat_channels
    )
    kernel = conv1_weight.reshape(27 * lat_channels, out_channels)
    result = jnp.dot(tap_columns, kernel, preferred_element_type=jnp.float32) + conv1_bias
    return result.astype(jnp.bfloat16).reshape(FR_DEV, TR_DEV, 2 * WT, out_channels)


def solution(mesh):
    return jax.shard_map(
        per_device,
        mesh=mesh,
        in_specs=(
            P("cfg", ("groups", "seq", "rows"), None),
            P(("groups", "seq", "rows")),
            P(("groups", "seq"), ("rows", "cfg"), None),
            P(),
            P(),
            P(),
            P(),
            P(),
            P(),
            P(),
            P(),
            P(),
            P(),
            P(),
        ),
        out_specs=P(("groups", "seq"), ("rows", "cfg"), None, None),
        check_vma=False,
    )
```

profile of v0, /device:TPU:1, one launch (start us, length us, event | category | flops | bytes accessed | tf_op | source)
XLA Modules:
  0.0 36.1 jit_solution(17837188760740041675)
XLA Ops:
  0.0 0.0 copy-start
  0.0 0.0 copy-start.1
  0.8 1.4 %fusion.30 = (s32[1]{0:T(128)}, s32[1]{0:T(128)}) fusion(s32[9]{0:T(128)} %param.21, s32[]{:T(128)S(6)} %select_n.38, s32[]{:T(128)S(6)} %select_n.37), kind=kLoop, calls=%fused_computation.73 | loop fusion | bytes 24 | tf_op jit(solution)/shard_map/dynamic_slice | solution.py:90
  3.5 0.9 %slice_add_fusion = (f32[1,5120]{1,0:T(1,128)S(1)}, f32[1,5120]{1,0:T(1,128)S(1)}) fusion(f32[2,5120]{1,0:T(2,128)} %param.18), kind=kLoop, calls=%fused_computation.26 | loop fusion | flops 5120 | bytes 81920 | tf_op jit(solution)/shard_map/add | solution.py:35
  4.4 0.0 copy-start.3
  4.4 2.2 %convert_reduce_fusion = f32[256]{0:T(256)S(1)} fusion(bf16[1,256,5120]{2,1,0:T(8,128)(2,1)} %param.14), kind=kLoop, calls=%fused_computation.1 | loop fusion | flops 2621184 | bytes 2622464 | tf_op jit(solution)/shard_map/reduce_sum | solution.py:32
  6.6 0.0 copy-done.1
  6.6 0.8 %fusion.3 = f32[256]{0:T(256)S(1)} fusion(bf16[1,256,5120]{2,1,0:T(8,128)(2,1)S(1)} %copy-done.1, f32[256]{0:T(256)S(1)} %broadcast_multiply_fusion), kind=kLoop, calls=%fused_computation.6 | loop fusion | flops 5242624 | bytes 2623488 | tf_op jit(solution)/shard_map/reduce_sum | solution.py:33
  7.4 0.0 copy-done.3
  7.5 0.0 copy-done
  7.5 0.0 copy-start.2
  7.5 1.1 %fusion.7 = f32[256,64]{1,0:T(8,128)S(1)} fusion(bf16[5120,64]{0,1:T(8,128)(2,1)S(1)} %copy-done, bf16[1,256,5120]{2,1,0:T(8,128)(2,1)S(1)} %copy-done.1, f32[5120]{0:T(1024)S(1)} %bitcast.57, f32[5120]{0:T(1024)S(1)} %bitcast.56, f32[256]{0:T(256)S(1)} %add_rsqrt_fusion, f32[256]{0:T(256)S(1)} %broadcast_multiply_fusion), kind=kOutput, calls=%fused_computation.10 | convolution fusion | flops 175636480 | bytes 3385344 | tf_op jit(solution)/shard_map/dot_general | solution.py:36
  8.6 0.0 copy-start.4
  8.7 0.0 copy-start.6
  8.7 0.0 copy-start.7
  8.7 0.0 copy-start.8
  8.7 1.2 %scatter_custom_fusion = f32[256,64]{1,0:T(8,128)S(1)} fusion(s32[256]{0:T(256)S(1)} %compare_select_fusion, f32[256,64]{1,0:T(8,128)S(1)} %fusion.7, f32[]{:T(128)} %constant.82.clone.1), kind=kCustom, calls=%fused_computation.16 | custom fusion | bytes 65540 | tf_op jit(solution)/shard_map/scatter | solution.py:81
  9.9 0.1 copy.30
  10.0 0.1 reshape.49
  10.1 0.3 copy.31
  10.4 0.7 %broadcast_in_dim_reshape.3 = f32[1,2,2,2,2048]{4,3,2,1,0:T(2,128)S(1)} reshape(f32[2,2,2,64,2,16]{5,4,3,2,1,0:T(2,128)S(1)} %copy.31) | data formatting | bytes 131072 | tf_op jit(solution)/shard_map/broadcast_in_dim;reshape | solution.py:84
  11.1 1.9 %all_gather.3 = f32[2,2,2,2,2048]{4,3,2,1,0:T(2,128)S(1)} all-gather(f32[1,2,2,2,2048]{4,3,2,1,0:T(2,128)S(1)} %broadcast_in_dim_reshape.3), channel_id=1, replica_groups=mesh['groups'=2,'seq'=4,'rows'=2,'cfg'=2] {'cfg'}, dimensions={0}, use_global_device_ids=true | all-gather | bytes 196608 | tf_op jit(solution)/shard_map/all_gather | solution.py:84
  13.6 0.0 copy-done.2
  13.7 0.1 reshape.50
  13.8 0.1 copy.32
  13.9 0.0 copy-done.4
  13.9 0.0 copy-done.6
  13.9 0.0 copy-done.7
  13.9 0.0 copy-done.8
  14.0 0.2 fusion.10
  14.2 0.1 copy.34
  14.3 0.2 reshape.51
  14.5 4.5 %collective-permute-start = (bf16[2,1,2048]{2,1,0:T(2,128)(2,1)S(1)}, bf16[2,1,2048]{2,1,0:T(2,128)(2,1)S(1)}, u32[]{:S(2)}, u32[]{:S(2)}) collective-permute-start(bf16[2,1,2048]{2,1,0:T(2,128)(2,1)S(1)} %get-tuple-element.36), channel_id=1, source_target_pairs={{0,1},{1,2},{2,3},{4,5},{5,6},{6,7},{8,9},{9,10},{10,11},{12,13},{... | collective-permute-start | bytes 24584 | tf_op jit(solution)/shard_map/ppermute | solution.py:16
  19.0 1.9 %collective-permute-start.1 = (bf16[2,1,2048]{2,1,0:T(2,128)(2,1)S(1)}, bf16[2,1,2048]{2,1,0:T(2,128)(2,1)S(1)}, u32[]{:S(2)}, u32[]{:S(2)}) collective-permute-start(bf16[2,1,2048]{2,1,0:T(2,128)(2,1)S(1)} %get-tuple-element.37), channel_id=1, source_target_pairs={{1,0},{2,1},{3,2},{5,4},{6,5},{7,6},{9,8},{10,9},{11,10},{13,12},{... | collective-permute-start | bytes 24584 | tf_op jit(solution)/shard_map/ppermute | solution.py:19
  21.0 0.0 collective-permute-done
  21.0 3.1 %collective-permute-done.1 = bf16[2,1,2048]{2,1,0:T(2,128)(2,1)S(1)} collective-permute-done((bf16[2,1,2048]{2,1,0:T(2,128)(2,1)S(1)}, bf16[2,1,2048]{2,1,0:T(2,128)(2,1)S(1)}, u32[]{:S(2)}, u32[]{:S(2)}) %collective-permute-start.1) | collective-permute-done | bytes 8224 | tf_op jit(solution)/shard_map/ppermute | solution.py:19
  24.1 0.1 pad_maximum_fusion
  24.2 3.2 %collective-permute-start.2 = (bf16[2,4,2048]{2,1,0:T(4,128)(2,1)S(1)}, bf16[2,4,2048]{2,1,0:T(4,128)(2,1)S(1)}, u32[]{:S(2)}, u32[]{:S(2)}) collective-permute-start(bf16[2,4,2048]{2,1,0:T(4,128)(2,1)S(1)} %pad_maximum_fusion), channel_id=1, source_target_pairs={{0,4},{4,8},{8,12},{1,5},{5,9},{9,13},{2,6},{6,10},{10,14},{3,7},{... | collective-permute-start | bytes 98312 | tf_op jit(solution)/shard_map/ppermute | solution.py:27
  27.4 1.0 %collective-permute-done.2 = bf16[2,4,2048]{2,1,0:T(4,128)(2,1)S(1)} collective-permute-done((bf16[2,4,2048]{2,1,0:T(4,128)(2,1)S(1)}, bf16[2,4,2048]{2,1,0:T(4,128)(2,1)S(1)}, u32[]{:S(2)}, u32[]{:S(2)}) %collective-permute-start.2) | collective-permute-done | bytes 32800 | tf_op jit(solution)/shard_map/ppermute | solution.py:27
  28.4 0.1 maximum_maximum_fusion
  28.5 0.4 %reshape.52 = bf16[4,4,128,16]{3,2,1,0:T(8,128)(2,1)S(1)} reshape(bf16[4,4,2048]{2,1,0:T(4,128)(2,1)S(1)} %maximum_maximum_fusion) | data formatting | bytes 131072 | tf_op jit(solution)/shard_map/reshape | solution.py:101
  28.8 0.3 pad_slice_fusion.1
  29.1 1.0 %pad_slice_fusion = (bf16[2,2,128,16]{3,2,1,0:T(8,128)(2,1)S(1)}, bf16[2,2,128,16]{3,2,1,0:T(8,128)(2,1)S(1)}, bf16[2,2,128,16]{3,2,1,0:T(8,128)(2,1)S(1)}, bf16...) fusion(bf16[4,4,128,16]{3,2,1,0:T(8,128)(2,1)S(1)} %reshape.52), kind=kLoop, calls=%fused_computation.52 | loop fusion | bytes 819200 | tf_op jit(solution)/shard_map/slice | solution.py:45
  30.1 0.0 copy-start.5
  30.1 0.9 %fusion.27 = (bf16[2,2,128,16]{3,2,1,0:T(8,128)(2,1)}, bf16[2,2,128,16]{3,2,1,0:T(8,128)(2,1)}, bf16[2,2,128,16]{3,2,1,0:T(8,128)(2,1)}, bf16[2,2,128,16]{3,2,1,...) fusion(bf16[4,4,128,16]{3,2,1,0:T(8,128)(2,1)S(1)} %reshape.52), kind=kLoop, calls=%fused_computation.70 | loop fusion | bytes 1277952 | tf_op jit(solution)/shard_map/slice | solution.py:45
  31.0 2.9 %concatenate.11 = bf16[2,2,128,432]{3,2,1,0:T(8,128)(2,1)S(1)} concatenate(bf16[2,2,128,16]{3,2,1,0:T(8,128)(2,1)} %get-tuple-element.31, bf16[2,2,128,16]{3,2,1,0:T(8,128)(2,1)} %get-tuple-element.30, bf16[2,2,128,16]{3,2,1,0:T(8,128)(2,1)S(1)} %get-tuple-element.6, bf16[2,2,128,16]{3,2,1,0:T(8,128)(2,1)S(1)} %get-tuple-element.7, bf16[2,2,128,16]{3,2,1,0:T(8,128)(2,1)} %get-tuple-element.29, ...), dimensions={3} | concatenate | bytes 884736 | tf_op jit(solution)/shard_map/concatenate | solution.py:52
  33.9 0.0 copy-done.5
  33.9 2.2 %fusion.9 = bf16[512,384]{1,0:T(8,128)(2,1)} fusion(bf16[512,432]{1,0:T(8,128)(2,1)S(1)} %bitcast.55, bf16[432,384]{1,0:T(8,128)(2,1)} %bitcast.58, f32[384]{0:T(512)S(1)} %copy-done.5), kind=kOutput, calls=%fused_computation.12 | convolution fusion | flops 170262528 | bytes 1168896 | tf_op jit(solution)/shard_map/dot_general | solution.py:109
  (6 shorter events, 0.1 us)
Async XLA Ops:
  0.0 7.5 %copy-start = (bf16[5120,64]{0,1:T(8,128)(2,1)S(1)}, bf16[5120,64]{0,1:T(8,128)(2,1)}, u32[]{:S(2)}) copy-start(bf16[5120,64]{0,1:T(8,128)(2,1)} %param.17) | copy-start | bytes 1966084
  0.0 6.6 %copy-start.1 = (bf16[1,256,5120]{2,1,0:T(8,128)(2,1)S(1)}, bf16[1,256,5120]{2,1,0:T(8,128)(2,1)}, u32[]{:S(2)}) copy-start(bf16[1,256,5120]{2,1,0:T(8,128)(2,1)} %param.14) | copy-start | bytes 7864324
  4.4 3.0 %copy-start.3 = (s32[256]{0:T(256)S(1)}, s32[256]{0:T(256)}, u32[]{:S(2)}) copy-start(s32[256]{0:T(256)} %param.15) | copy-start | bytes 3076
  7.5 6.2 %copy-start.2 = (f32[2,2,2048]{2,1,0:T(2,128)S(1)}, f32[2,2,2048]{2,1,0:T(2,128)}, u32[]{:S(2)}) copy-start(f32[2,2,2048]{2,1,0:T(2,128)} %param.16) | copy-start | bytes 98308
  8.6 5.3 %copy-start.4 = (f32[16,16]{1,0:T(8,128)S(1)}, f32[16,16]{1,0:T(8,128)}, u32[]{:S(2)}) copy-start(f32[16,16]{1,0:T(8,128)} %param.24) | copy-start | bytes 3076
  8.7 5.3 %copy-start.6 = (f32[16]{0:T(128)S(1)}, f32[16]{0:T(128)}, u32[]{:S(2)}) copy-start(f32[16]{0:T(128)} %param.25) | copy-start | bytes 196
  8.7 5.3 %copy-start.7 = (f32[16]{0:T(128)S(1)}, f32[16]{0:T(128)}, u32[]{:S(2)}) copy-start(f32[16]{0:T(128)} %param.22) | copy-start | bytes 196
  8.7 5.3 %copy-start.8 = (f32[16]{0:T(128)S(1)}, f32[16]{0:T(128)}, u32[]{:S(2)}) copy-start(f32[16]{0:T(128)} %param.23) | copy-start | bytes 196
  14.5 6.4 %collective-permute-start = (bf16[2,1,2048]{2,1,0:T(2,128)(2,1)S(1)}, bf16[2,1,2048]{2,1,0:T(2,128)(2,1)S(1)}, u32[]{:S(2)}, u32[]{:S(2)}) collective-permute-start(bf16[2,1,2048]{2,1,0:T(2,128)(2,1)S(1)} %get-tuple-element.36), channel_id=1, source_target_pairs={{0,1},{1,2},{2,3},{4,5},{5,6},{6,7},{8,9},{9,10},{10,11},{12,13},{... | collective-permute-start | bytes 24584 | tf_op jit(solution)/shard_map/ppermute | solution.py:16
  19.0 5.1 %collective-permute-start.1 = (bf16[2,1,2048]{2,1,0:T(2,128)(2,1)S(1)}, bf16[2,1,2048]{2,1,0:T(2,128)(2,1)S(1)}, u32[]{:S(2)}, u32[]{:S(2)}) collective-permute-start(bf16[2,1,2048]{2,1,0:T(2,128)(2,1)S(1)} %get-tuple-element.37), channel_id=1, source_target_pairs={{1,0},{2,1},{3,2},{5,4},{6,5},{7,6},{9,8},{10,9},{11,10},{13,12},{... | collective-permute-start | bytes 24584 | tf_op jit(solution)/shard_map/ppermute | solution.py:19
  24.2 4.2 %collective-permute-start.2 = (bf16[2,4,2048]{2,1,0:T(4,128)(2,1)S(1)}, bf16[2,4,2048]{2,1,0:T(4,128)(2,1)S(1)}, u32[]{:S(2)}, u32[]{:S(2)}) collective-permute-start(bf16[2,4,2048]{2,1,0:T(4,128)(2,1)S(1)} %pad_maximum_fusion), channel_id=1, source_target_pairs={{0,4},{4,8},{8,12},{1,5},{5,9},{9,13},{2,6},{6,10},{10,14},{3,7},{... | collective-permute-start | bytes 98312 | tf_op jit(solution)/shard_map/ppermute | solution.py:27
  30.1 3.8 %copy-start.5 = (f32[384]{0:T(512)S(1)}, f32[384]{0:T(512)}, u32[]{:S(2)}) copy-start(f32[384]{0:T(512)} %param.27) | copy-start | bytes 4612
where the time goes:
time: 36.6 us; the launch traced here: 36.1 us
  local copies, waits for them, and re-layouts  9.76 us (27%)
  starting transfers between devices  9.62 us (26%)
  waiting for transfers between devices  4.13 us (11%)
  other arithmetic  4.12 us (11%)
  matrix products  3.55 us (10%)
  between operations  2.99 us (8%)
  blocking collectives  1.9 us (5%)
    ppermute x1, starting transfers between devices, padded_2(): lax.ppermute(lax.slice_in_dim(block, block.shape[dim] - width, None, axis...  4.5 us
    ppermute x1, starting transfers between devices, shifted(): return lax.ppermute(block, axis, route)  3.2 us
    ppermute x1, waiting for transfers between devices, padded_2(): lax.ppermute(lax.slice_in_dim(block, 0, width, axis=dim), axis, backward)  3.12 us
    concatenate x1, local copies, waits for them, and re-layouts, conv_taps(): return jnp.concatenate(pieces, axis=-1)  2.88 us
    reduce_sum x1, other arithmetic, head_rows(): center = jnp.mean(values, axis=-1, keepdims=True)  2.18 us
    slice x3, local copies, waits for them, and re-layouts, conv_taps(): padded[step_time:step_time + frames, step_row:step_row + row_count, step_...  2.17 us
    dot_general x1, matrix products, per_device(): jnp.dot(tap_columns, kernel, preferred_element_type=jnp.float32)  2.16 us
    ppermute x1, starting transfers between devices, padded_2(): lax.ppermute(lax.slice_in_dim(block, 0, width, axis=dim), axis, backward)  1.92 us
  transfers between devices with their start and end apart: 3, of which 2 were waited for; matrix products, arithmetic and copies ran while one was open for 0% of the time, Pallas kernels for 0%

commit v1 on v0

v1 whole, which is shorter than its diff:
```python
import functools

import jax
import jax.numpy as jnp
from jax import lax
from jax.experimental import pallas as pl
from jax.experimental.pallas import tpu as pltpu
from jax.sharding import PartitionSpec as P

HIGHEST = lax.Precision.HIGHEST
F32 = jnp.float32
BF16 = jnp.bfloat16
NN = (((1,), (0,)), ((), ()))
NT = (((1,), (1,)), ((), ()))
TN = (((0,), (0,)), ((), ()))
RING = ("seq", "rows", "cfg")


def mm(left, right, dims=NN, precision=None):
    return lax.dot_general(left, right, dims, precision=precision, preferred_element_type=F32)


def iota(shape, dim):
    return lax.broadcasted_iota(jnp.int32, shape, dim)


def head_kernel(
    hid, wt, mod, tok, noisy, mean, std, w2, b2,
    out,
    x_v, w_v, mod_v, tok_v, noisy_v, mean_v, std_v, w2_v, b2_v,
    wcat_v, place_v, mask_v, square_v, pivot_v, small_sem, w_sem, x_sem,
):
    tokens, width = x_v.shape
    outs = w_v.shape[0]
    chans = w2_v.shape[0]
    frames, token_rows, row_lanes = noisy_v.shape
    cols = row_lanes // chans
    cells = 2 * tokens
    chunks = x_sem.shape[0]
    chunk = width // chunks
    pairs = [
        (tok, tok_v), (w2, w2_v), (mean, mean_v), (std, std_v), (b2, b2_v), (noisy, noisy_v),
    ]
    small = [pltpu.make_async_copy(a, b, small_sem.at[i]) for i, (a, b) in enumerate(pairs)]
    big = [pltpu.make_async_copy(mod, mod_v, w_sem.at[0]), pltpu.make_async_copy(wt, w_v, w_sem.at[1])]
    loads = []
    for k in range(chunks):
        span = pl.ds(k * chunk, chunk)
        loads.append(pltpu.make_async_copy(hid.at[:, span], x_v.at[:, span], x_sem.at[k]))
    for copy in small + big + loads:
        copy.start()
    for copy in small:
        copy.wait()

    frame_cells = lax.axis_size("rows") * token_rows * (cols // 2)
    cell = tok_v[...] - lax.axis_index("seq") * frames * frame_cells
    late = jnp.zeros_like(cell)
    for f in range(1, frames):
        late = late + (cell >= f * frame_cells).astype(jnp.int32)
    local = (
        cell - late * frame_cells - lax.axis_index("rows") * token_rows * (cols // 2)
        + late * token_rows * (cols // 2)
    )
    block = 128
    for e in range(2):
        target = 2 * local + e
        for start in range(0, cells, block):
            hit = iota((block, tokens), 0) + start == target
            place_v[pl.ds(start, block), pl.ds(e * tokens, tokens)] = jnp.where(hit, 1.0, 0.0).astype(BF16)

    lanes = 128
    reps = lanes // chans
    spread = (iota((chans, lanes), 1) % chans == iota((chans, lanes), 0)).astype(F32)
    row8 = iota((8, chans), 0)
    stacked = jnp.where(row8 == 0, std_v[...], jnp.where(row8 == 1, mean_v[...], b2_v[...]))
    tiled = mm(stacked, spread, NN, HIGHEST)
    mix = mm(w2_v[...], spread, TN, HIGHEST)
    diag = jnp.where(iota((chans, lanes), 1) == iota((chans, lanes), 0), tiled[2:3], 0.0)
    offset = jnp.sum(
        jnp.where(iota((chans, lanes), 1) < chans, mix * tiled[1:2] + diag, 0.0), axis=1, keepdims=True
    )
    mix = mix * tiled[0:1]

    own = iota((reps, lanes), 1) // chans == iota((reps, lanes), 0)
    tail = frames * token_rows * token_rows * chans
    for a in range(token_rows):
        for f in range(frames):
            for j in range(row_lanes // lanes):
                piece = noisy_v[f, a : a + 1, j * lanes : (j + 1) * lanes]
                mask_v[pl.ds(f * cols + j * reps, reps), :] = jnp.where(own, piece, 0.0)
        noise = mm(mix, mask_v[...], NT, HIGHEST) + offset
        for f in range(frames):
            at = tail + (f * token_rows + a) * chans
            out[pl.ds(at, chans), :] = noise[:, f * cols : (f + 1) * cols]

    blocks = outs // chans
    spot_o = iota((outs, outs), 0) // chans
    spot_j = iota((outs, outs), 1) // chans
    match = (spot_o % 2 == spot_j // 2) & (spot_o // 2 == spot_j % 2)
    mixer = jnp.where(match, jnp.concatenate([mix[:, :outs]] * blocks, axis=0), 0.0)

    for copy in big:
        copy.wait()
    piece = 512
    col_sum = jnp.zeros((outs, lanes), F32)
    shift_sum = jnp.zeros((outs, lanes), F32)
    for start in range(0, width, piece):
        span = pl.ds(start, piece)
        weight = w_v[:, span].astype(F32)
        scaled = weight * (1.0 + mod_v[1:2, span])
        high = scaled.astype(BF16)
        wcat_v[0:outs, span] = high
        wcat_v[outs : 2 * outs, span] = (scaled - high.astype(F32)).astype(BF16)
        shifted = weight * mod_v[0:1, span]
        for j in range(0, piece, lanes):
            col_sum = col_sum + scaled[:, j : j + lanes]
            shift_sum = shift_sum + shifted[:, j : j + lanes]
    wcat_v[2 * outs :, :] = jnp.ones((wcat_v.shape[0] - 2 * outs, width), BF16)
    col_sum = jnp.sum(col_sum, axis=1, keepdims=True)
    shift_sum = jnp.sum(shift_sum, axis=1, keepdims=True)

    group = 32
    total = jnp.zeros((wcat_v.shape[0], tokens), F32)
    for k in range(chunks):
        loads[k].wait()
        span = pl.ds(k * chunk, chunk)
        total = total + mm(wcat_v[:, span], x_v[:, span], NT)
        for g in range(0, tokens, group):
            rows = pl.ds(g, group)
            values = x_v[rows, span].astype(F32)
            if k == 0:
                pivot = jnp.sum(values[:, :lanes], axis=1, keepdims=True) * (1.0 / lanes)
                pivot = jnp.broadcast_to(pivot, (group, lanes))
                pivot_v[rows, :] = pivot
                squares = jnp.zeros((group, lanes), F32)
            else:
                pivot = pivot_v[rows, :]
                squares = square_v[rows, :]
            for j in range(0, chunk, lanes):
                gap = values[:, j : j + lanes] - pivot
                squares = squares + gap * gap
            square_v[rows, :] = squares

    square = mm(jnp.ones((8, lanes), F32), square_v[...], NT, HIGHEST)[0:1] * (1.0 / width)
    pivot = mm(jnp.ones((8, lanes), F32), pivot_v[...], NT, HIGHEST)[0:1] * (1.0 / lanes)
    center = total[2 * outs : 2 * outs + 1] * (1.0 / width)
    gap = center - pivot
    inverse = lax.rsqrt(jnp.maximum(square - gap * gap, 0.0) + 1e-06)
    head = (total[0:outs] + total[outs : 2 * outs] - center * col_sum) * inverse + shift_sum
    mixed = mm(mixer, head, NN, HIGHEST)
    side = outs // 2
    mixed = jnp.concatenate([mixed[:side], mixed[side:]], axis=1)
    high = mixed.astype(BF16)
    rest = mixed - high.astype(F32)
    middle = rest.astype(BF16)
    low = (rest - middle.astype(F32)).astype(BF16)
    placed = mm(jnp.concatenate([high, middle, low], axis=0), place_v[...], NT)
    placed = placed[:side] + placed[side : 2 * side] + placed[2 * side :]
    for f in range(frames):
        for i in range(token_rows):
            at = f * token_rows + i
            out[pl.ds(at * side, side), :] = placed[:, at * cols : (at + 1) * cols]


def head_call(hidden, token_order, noisy, head_weight, head_mod, mean, std, w2, b2):
    tokens, width = hidden.shape[1:]
    outs = head_weight.shape[1]
    chans = w2.shape[0]
    frames, rows, row_lanes = noisy.shape
    cols = row_lanes // chans
    chunks = 5
    hbm = pl.BlockSpec(memory_space=pl.ANY)
    vmem = pltpu.VMEM
    return pl.pallas_call(
        head_kernel,
        out_shape=jax.ShapeDtypeStruct((frames * rows * (rows + 1) * chans, cols), F32),
        in_specs=[hbm] * 9,
        out_specs=pl.BlockSpec(memory_space=pltpu.VMEM),
        scratch_shapes=[
            vmem((tokens, width), BF16), vmem((outs, width), BF16), vmem((2, width), F32),
            vmem((1, tokens), jnp.int32), vmem(noisy.shape, F32),
            vmem((1, chans), F32), vmem((1, chans), F32), vmem(w2.shape, F32), vmem((1, chans), F32),
            vmem((2 * outs + 16, width), BF16), vmem((2 * tokens, 2 * tokens), BF16),
            vmem((frames * cols, 128), F32), vmem((tokens, 128), F32), vmem((tokens, 128), F32),
            pltpu.SemaphoreType.DMA((6,)), pltpu.SemaphoreType.DMA((2,)), pltpu.SemaphoreType.DMA((chunks,)),
        ],
        compiler_params=limit(20),
        name="head",
    )(
        *(
            pltpu.with_memory_space_constraint(value, pltpu.HBM)
            for value in (
                hidden.reshape(tokens, width), head_weight.T, head_mod, token_order.reshape(1, -1), noisy,
                mean.reshape(1, -1), std.reshape(1, -1), w2, b2.reshape(1, -1),
            )
        )
    )


def merge_kernel(frames, token_rows, by_half, mine, theirs, guide, step, table, own, edge):
    half = lax.axis_index("cfg")
    side = own.shape[0] // (frames * token_rows)
    chans = edge.shape[0] // frames
    tail = own.shape[0]
    gaps = iota(table.shape, 1) - step[0]
    gaps = jnp.where(gaps == 1, table[...], jnp.where(gaps == 0, -table[...], 0))
    delta = jnp.sum(gaps.astype(F32), axis=1, keepdims=True) * (1.0 / 1000.0)
    cond = guide[0] * delta
    uncond = delta - cond
    left = jnp.where(half == 0, cond, uncond)
    right = jnp.where(half == 0, uncond, cond)
    lower = half == 1 if by_half else lax.axis_index("rows") == 0
    for f in range(frames):
        spot = pl.ds(tail + f * side, side)
        near, far = mine[spot, :], theirs[spot, :]
        values = []
        for i in range(token_rows):
            at = pl.ds((f * token_rows + i) * side, side)
            value = left * mine[at, :] + right * theirs[at, :] + jnp.where(half == i, near, far)
            value = value.astype(BF16)
            own[at, :] = value
            values.append(value)
        edge[pl.ds(f * chans, chans), :] = jnp.where(lower, values[-1][side - chans :], values[0][:chans])


def merge_call(mine, theirs, guidance, index, table, frames, token_rows, chans, by_half):
    tall = frames * token_rows * token_rows * chans
    cols = mine.shape[1]
    vmem = pl.BlockSpec(memory_space=pltpu.VMEM)
    smem = pl.BlockSpec(memory_space=pltpu.SMEM)
    return pl.pallas_call(
        functools.partial(merge_kernel, frames, token_rows, by_half),
        out_shape=(
            jax.ShapeDtypeStruct((tall, cols), BF16),
            jax.ShapeDtypeStruct((frames * chans, cols), BF16),
        ),
        in_specs=[vmem, vmem, smem, smem, vmem],
        out_specs=(vmem, vmem),
        compiler_params=limit(4),
        name="merge",
    )(mine, theirs, guidance, index, table.reshape(1, -1))


def limit(mebibytes):
    return pltpu.CompilerParams(vmem_limit_bytes=mebibytes * 2**20)


def widen_kernel(rows, weight, after, wide):
    taps, chans, chans_out = weight.shape
    span = rows + 2
    depth = span * chans
    for t in range(3):
        for w in range(3):
            for y in range(rows):
                for q in range(span):
                    u = q - y
                    if 0 <= u < 3:
                        value = weight[9 * t + 3 * u + w]
                    else:
                        value = jnp.zeros((chans, chans_out), BF16)
                    wide[w, pl.ds(t * depth + q * chans, chans), pl.ds(y * chans_out, chans_out)] = value


def widen_call(weight, after, rows):
    taps, chans, chans_out = weight.shape
    vmem = pl.BlockSpec(memory_space=pltpu.VMEM)
    return pl.pallas_call(
        functools.partial(widen_kernel, rows),
        out_shape=jax.ShapeDtypeStruct((3, 3 * (rows + 2) * chans, rows * chans_out), BF16),
        in_specs=[vmem, pl.BlockSpec(memory_space=pl.ANY)],
        out_specs=vmem,
        compiler_params=limit(8),
        name="widen",
    )(weight, after)


def conv_kernel(
    own, near, prev, prev_near, wide_v, bias,
    out,
    stack_v,
):
    frames, rows, cols, chans_out = out.shape
    depth = wide_v.shape[1] // 3
    chans = depth // (rows + 2)
    half = lax.axis_index("cfg")
    row = lax.axis_index("rows")
    past = lax.axis_index("seq") > 0
    inner = jnp.where(half == 0, row > 0, row < lax.axis_size("rows") - 1)
    first = half == 0
    band = 2 * rows * chans
    zero = jnp.zeros((chans, cols), BF16)
    tail = frames * band
    for f in range(2 * frames):
        if f < frames:
            at = pl.ds(f * band, band)
            base = jnp.where(first, prev_near[at, :], prev[at, :])
            base = jnp.where(past, base, jnp.zeros_like(base))
            at = pl.ds(tail + f * chans, chans)
            edge = jnp.where(first, prev_near[at, :], prev[at, :])
            edge = jnp.where(past & inner, edge, zero)
        else:
            base = own[pl.ds((f - frames) * band, band), :]
            edge = jnp.where(inner, near[pl.ds((f - frames) * chans, chans), :], zero)
        keep = (rows + 1) * chans
        stack_v[pl.ds(f * depth, depth), :] = jnp.where(
            first,
            jnp.concatenate([edge, base[:keep]], axis=0),
            jnp.concatenate([base[band - keep :], edge], axis=0),
        )
    latents = stack_v[...]
    shifted = []
    for w in range(3):
        pick = (iota((cols, cols), 0) + (w - 1) == iota((cols, cols), 1)).astype(F32).astype(BF16)
        shifted.append(mm(pick, latents, NT).astype(BF16))
    for f in range(frames):
        window = slice(f * depth, (f + 3) * depth)
        total = mm(shifted[0][:, window], wide_v[0])
        for w in range(1, 3):
            total = total + mm(shifted[w][:, window], wide_v[w])
        for y in range(rows):
            value = total[:, y * chans_out : (y + 1) * chans_out] + bias[...]
            out[f, y] = value.astype(BF16)


def conv_call(own, near, prev, prev_near, wide, bias, frames, rows):
    cols = own.shape[1]
    depth = wide.shape[1] // 3
    chans_out = wide.shape[2] // rows
    vmem = pl.BlockSpec(memory_space=pltpu.VMEM)
    return pl.pallas_call(
        conv_kernel,
        out_shape=jax.ShapeDtypeStruct((frames, rows, cols, chans_out), BF16),
        in_specs=[vmem] * 6,
        out_specs=vmem,
        scratch_shapes=[pltpu.VMEM((2 * frames * depth, cols), BF16)],
        compiler_params=limit(8),
        name="conv",
    )(own, near, prev, prev_near, wide, bias)


def routes(sizes, rule):
    seqs, rows, halves = sizes
    pairs = []
    for s in range(seqs):
        for r in range(rows):
            for c in range(halves):
                to = rule(s, r, c)
                if 0 <= to[0] < seqs and 0 <= to[1] < rows:
                    pairs.append(((s * rows + r) * halves + c, (to[0] * rows + to[1]) * halves + to[2]))
    return pairs


def send(value, sizes, rule):
    return lax.ppermute(value, RING, routes(sizes, rule))


def per_device(
    hidden,
    token_order,
    noisy_latent,
    head_weight,
    head_mod,
    guidance,
    timestep_index,
    step_table,
    vae_mean,
    vae_std,
    conv2_weight,
    conv2_bias,
    conv1_weight,
    conv1_bias,
):
    frames, rows, _ = noisy_latent.shape
    chans = conv2_weight.shape[0]
    sizes = tuple(lax.axis_size(axis) for axis in RING)
    seqs, row_count, _ = sizes
    part = head_call(
        hidden, token_order, noisy_latent, head_weight, head_mod, vae_mean, vae_std, conv2_weight, conv2_bias
    )
    other = send(part, sizes, lambda s, r, c: (s, r, 1 - c))
    own, edge = merge_call(
        part, other, guidance, timestep_index, step_table, frames, rows, chans, row_count != 2
    )
    if row_count == 2:
        top = seqs - 1

        def along(s, r, c):
            if c == 1:
                return (s + 1, r, 1) if s < top else (s, r, 0)
            return (s - 1, r, 0) if s > 0 else (s, r, 1)

        def across(s, r, c):
            if c == 1:
                return (s + 1, 1 - r, 1) if s < top else (s, 1 - r, 0)
            return (s - 1, r, 0) if s > 0 else (s, 1 - r, 1)

        prev = send(own, sizes, along)
        near = send(edge, sizes, lambda s, r, c: (s, 1 - r, c))
        prev_edge = send(edge, sizes, across)
        prev, near, prev_edge = lax.optimization_barrier((prev, near, prev_edge))
        prev = jnp.concatenate([prev, prev_edge], axis=0)
        prev_near = send(prev, sizes, lambda s, r, c: (s, r, 1 - c))
    else:
        near = send(edge, sizes, lambda s, r, c: (s, r - 1, 1) if c == 0 else (s, r + 1, 0))
        prev = send(own, sizes, lambda s, r, c: (s + 1, r, c))
        prev_edge = send(edge, sizes, lambda s, r, c: (s + 1, r - 1, 1) if c == 0 else (s + 1, r + 1, 0))
        prev = prev_near = jnp.concatenate([prev, prev_edge], axis=0)
    wide = widen_call(conv1_weight, edge, rows)
    return conv_call(own, near, prev, prev_near, wide, conv1_bias.reshape(1, -1), frames, rows)


def solution(mesh):
    return jax.shard_map(
        per_device,
        mesh=mesh,
        in_specs=(
            P("cfg", ("groups", "seq", "rows"), None),
            P(("groups", "seq", "rows")),
            P(("groups", "seq"), ("rows", "cfg"), None),
            P(),
            P(),
            P(),
            P(),
            P(),
            P(),
            P(),
            P(),
            P(),
            P(),
            P(),
        ),
        out_specs=P(("groups", "seq"), ("rows", "cfg"), None, None),
        check_vma=False,
    )
```

time: 36.6 us -> 18.1 us (0.49)
  the two profiles are of different devices: /device:TPU:1 before, /device:TPU:0 now
where the time goes in v1:
time: 18.1 us; the launch traced here: 18 us
  Pallas kernels  7.27 us (40%)
  starting transfers between devices  5.19 us (29%)
  waiting for transfers between devices  4.13 us (23%)
  between operations  1.34 us (7%)
    pallas_call x1, Pallas kernels, head_call(): pl.pallas_call(head_kernel, out_shape=jax.ShapeDtypeStruct((frames * rows...  5.64 us
    ppermute x5, starting transfers between devices, send(): return lax.ppermute(value, RING, routes(sizes, rule))  5.19 us
    ppermute x5, waiting for transfers between devices, send(): return lax.ppermute(value, RING, routes(sizes, rule))  4.13 us
    pallas_call x1, Pallas kernels, conv_call(): pl.pallas_call(conv_kernel, out_shape=jax.ShapeDtypeStruct((frames, rows,...  1.45 us
  transfers between devices with their start and end apart: 5, of which 3 were waited for; matrix products, arithmetic and copies ran while one was open for 0% of the time, Pallas kernels for 0%

profile of v1, /device:TPU:0, one launch (start us, length us, event | category | flops | bytes accessed | tf_op | source)
XLA Modules:
  0.0 18.0 jit_solution(318705107009804783)
XLA Ops:
  0.0 0.0 copy-start.1
  0.0 0.0 copy-start.2
  0.0 0.0 copy-start
  0.0 5.6 %head.1.mine = f32[192,128]{1,0:T(8,128)S(1)} custom-call(bf16[256,5120]{1,0:T(8,128)(2,1)} %bitcast.8, bf16[64,5120]{1,0:T(8,128)(2,1)} %bitcast.9, f32[2,5120]{1,0:T(2,128)} %mod.1, s32[1,256]{1,0:T(1,128)} %bitcast.10, f32[2,2,2048]{2,1,0:T(2,128)} %noisy.1, f32[1,16]{1,0:T(1,128)} %bitcast.11, f32[1,16]{1,0:T(1,128)} %bitcast.12, f32[16,16]{1,0:T(8,128)} %w2.1, ...), custom_call_target="tpu_custom_call" | custom-call | tf_op jit(solution)/shard_map/head/pallas_call | solution.py:174
  5.7 0.6 %collective-permute-start = (f32[192,128]{1,0:T(8,128)S(1)}, f32[192,128]{1,0:T(8,128)S(1)}, u32[]{:S(2)}, u32[]{:S(2)}) collective-permute-start(f32[192,128]{1,0:T(8,128)S(1)} %head.1.mine), channel_id=1, source_target_pairs={{0,1},{1,0},{2,3},{3,2},{4,5},{5,4},{6,7},{7,6},{8,9},{9,8},{10,11... | collective-permute-start | bytes 294920 | tf_op jit(solution)/shard_map/ppermute | solution.py:354
  7.5 0.0 collective-permute-done.theirs
  7.5 0.0 copy-done.1
  7.5 0.1 merge.1
  7.7 0.0 collective-permute-start.1
  7.7 3.9 %collective-permute-start.3 = (bf16[32,128]{1,0:T(8,128)(2,1)S(1)}, bf16[32,128]{1,0:T(8,128)(2,1)S(1)}, u32[]{:S(2)}, u32[]{:S(2)}) collective-permute-start(bf16[32,128]{1,0:T(8,128)(2,1)S(1)} %get-tuple-element.11.after), channel_id=1, source_target_pairs={{0,3},{1,7},{2,1},{3,5},{4,0},{5,11},{6,2},{7,9},{8,4},{9,15},{10,... | collective-permute-start | bytes 24584 | tf_op jit(solution)/shard_map/ppermute | solution.py:354
  11.6 0.5 %collective-permute-start.2 = (bf16[32,128]{1,0:T(8,128)(2,1)S(1)}, bf16[32,128]{1,0:T(8,128)(2,1)S(1)}, u32[]{:S(2)}, u32[]{:S(2)}) collective-permute-start(bf16[32,128]{1,0:T(8,128)(2,1)S(1)} %get-tuple-element.11.after), channel_id=1, source_target_pairs={{0,2},{1,3},{2,0},{3,1},{4,6},{5,7},{6,4},{7,5},{8,10},{9,11},{10,... | collective-permute-start | bytes 24584 | tf_op jit(solution)/shard_map/ppermute | solution.py:354
  12.1 0.8 %collective-permute-done.3 = bf16[32,128]{1,0:T(8,128)(2,1)S(1)} collective-permute-done((bf16[32,128]{1,0:T(8,128)(2,1)S(1)}, bf16[32,128]{1,0:T(8,128)(2,1)S(1)}, u32[]{:S(2)}, u32[]{:S(2)}) %collective-permute-start.3) | collective-permute-done | bytes 8224 | tf_op jit(solution)/shard_map/ppermute | solution.py:354
  12.9 2.3 %collective-permute-done.2.near = bf16[32,128]{1,0:T(8,128)(2,1)S(1)} collective-permute-done((bf16[32,128]{1,0:T(8,128)(2,1)S(1)}, bf16[32,128]{1,0:T(8,128)(2,1)S(1)}, u32[]{:S(2)}, u32[]{:S(2)}) %collective-permute-start.2) | collective-permute-done | bytes 8224 | tf_op jit(solution)/shard_map/ppermute | solution.py:354
  15.2 0.0 collective-permute-done.1
  15.2 0.2 collective-permute-start.4
  15.4 0.0 copy-done.2
  15.4 0.0 copy-done
  15.4 0.1 widen.1.wide_v
  15.5 1.0 %collective-permute-done.4.prev_near = bf16[160,128]{1,0:T(8,128)(2,1)S(1)} collective-permute-done((bf16[160,128]{1,0:T(8,128)(2,1)S(1)}, bf16[160,128]{1,0:T(8,128)(2,1)S(1)}, u32[]{:S(2)}, u32[]{:S(2)}) %collective-permute-start.4) | collective-permute-done | bytes 40992 | tf_op jit(solution)/shard_map/ppermute | solution.py:354
  16.5 1.4 %conv.1 = bf16[2,2,128,384]{3,2,1,0:T(8,128)(2,1)} custom-call(bf16[128,128]{1,0:T(8,128)(2,1)S(1)} %get-tuple-element.10.own, bf16[32,128]{1,0:T(8,128)(2,1)S(1)} %collective-permute-done.2.near, bf16[160,128]{1,0:T(8,128)(2,1)S(1)} %constant_dynamic-update-slice_fusion.prev, bf16[160,128]{1,0:T(8,128)(2,1)S(1)} %collective-permute-done.4.prev_near, ...), custom_call_target="tpu_custom_call" | custom-call | tf_op jit(solution)/shard_map/conv/pallas_call | solution.py:330
  (3 shorter events, 0.0 us)
Async XLA Ops:
  0.0 7.5 %copy-start.1 = (s32[9]{0:T(128)S(1)}, s32[9]{0:T(128)}, u32[]{:S(2)}) copy-start(s32[9]{0:T(128)} %param.21) | copy-start | bytes 112
  0.0 15.4 %copy-start.2 = (f32[384]{0:T(512)S(1)}, f32[384]{0:T(512)}, u32[]{:S(2)}) copy-start(f32[384]{0:T(512)} %param.27) | copy-start | bytes 4612
  0.0 15.4 %copy-start = (bf16[27,16,384]{2,1,0:T(8,128)(2,1)S(1)}, bf16[27,16,384]{2,1,0:T(8,128)(2,1)}, u32[]{:S(2)}) copy-start(bf16[27,16,384]{2,1,0:T(8,128)(2,1)} %weight.1) | copy-start | bytes 995332
  5.7 1.9 %collective-permute-start = (f32[192,128]{1,0:T(8,128)S(1)}, f32[192,128]{1,0:T(8,128)S(1)}, u32[]{:S(2)}, u32[]{:S(2)}) collective-permute-start(f32[192,128]{1,0:T(8,128)S(1)} %head.1.mine), channel_id=1, source_target_pairs={{0,1},{1,0},{2,3},{3,2},{4,5},{5,4},{6,7},{7,6},{8,9},{9,8},{10,11... | collective-permute-start | bytes 294920 | tf_op jit(solution)/shard_map/ppermute | solution.py:354
  7.7 7.6 %collective-permute-start.1 = (bf16[128,128]{1,0:T(8,128)(2,1)S(1)}, bf16[128,128]{1,0:T(8,128)(2,1)S(1)}, u32[]{:S(2)}, u32[]{:S(2)}) collective-permute-start(bf16[128,128]{1,0:T(8,128)(2,1)S(1)} %get-tuple-element.10.own), channel_id=1, source_target_pairs={{0,1},{1,5},{2,3},{3,7},{4,0},{5,9},{6,2},{7,11},{8,4},{9,13},{10,... | collective-permute-start | bytes 98312 | tf_op jit(solution)/shard_map/ppermute | solution.py:354
  7.7 5.2 %collective-permute-start.3 = (bf16[32,128]{1,0:T(8,128)(2,1)S(1)}, bf16[32,128]{1,0:T(8,128)(2,1)S(1)}, u32[]{:S(2)}, u32[]{:S(2)}) collective-permute-start(bf16[32,128]{1,0:T(8,128)(2,1)S(1)} %get-tuple-element.11.after), channel_id=1, source_target_pairs={{0,3},{1,7},{2,1},{3,5},{4,0},{5,11},{6,2},{7,9},{8,4},{9,15},{10,... | collective-permute-start | bytes 24584 | tf_op jit(solution)/shard_map/ppermute | solution.py:354
  11.6 3.7 %collective-permute-start.2 = (bf16[32,128]{1,0:T(8,128)(2,1)S(1)}, bf16[32,128]{1,0:T(8,128)(2,1)S(1)}, u32[]{:S(2)}, u32[]{:S(2)}) collective-permute-start(bf16[32,128]{1,0:T(8,128)(2,1)S(1)} %get-tuple-element.11.after), channel_id=1, source_target_pairs={{0,2},{1,3},{2,0},{3,1},{4,6},{5,7},{6,4},{7,5},{8,10},{9,11},{10,... | collective-permute-start | bytes 24584 | tf_op jit(solution)/shard_map/ppermute | solution.py:354
  15.2 1.3 %collective-permute-start.4 = (bf16[160,128]{1,0:T(8,128)(2,1)S(1)}, bf16[160,128]{1,0:T(8,128)(2,1)S(1)}, u32[]{:S(2)}, u32[]{:S(2)}) collective-permute-start(bf16[160,128]{1,0:T(8,128)(2,1)S(1)} %constant_dynamic-update-slice_fusion.prev), channel_id=1, source_target_pairs={{0,1},{1,0},{2,3},{3,2},{4,5},{5,4},{6,7},{7,6},{8,9},{9,8},{10,11... | collective-permute-start | bytes 122888 | tf_op jit(solution)/shard_map/ppermute | solution.py:354

commit v2 on v1

--- a/solution.py
+++ b/solution.py
@@ -6,6 +6,7 @@
 from jax.experimental import pallas as pl
 from jax.experimental.pallas import tpu as pltpu
 from jax.sharding import PartitionSpec as P
+
 
 HIGHEST = lax.Precision.HIGHEST
 F32 = jnp.float32
@@ -47,7 +48,7 @@
     for k in range(chunks):
         span = pl.ds(k * chunk, chunk)
         loads.append(pltpu.make_async_copy(hid.at[:, span], x_v.at[:, span], x_sem.at[k]))
-    for copy in small + big + loads:
+    for copy in small + big + loads[:1]:
         copy.start()
     for copy in small:
         copy.wait()
@@ -101,6 +102,8 @@
 
     for copy in big:
         copy.wait()
+    for copy in loads[1:5]:
+        copy.start()
     piece = 512
     col_sum = jnp.zeros((outs, lanes), F32)
     shift_sum = jnp.zeros((outs, lanes), F32)
@@ -123,6 +126,8 @@
     total = jnp.zeros((wcat_v.shape[0], tokens), F32)
     for k in range(chunks):
         loads[k].wait()
+        for copy in loads[5:] if k == 0 else ():
+            copy.start()
         span = pl.ds(k * chunk, chunk)
         total = total + mm(wcat_v[:, span], x_v[:, span], NT)
         for g in range(0, tokens, group):
@@ -246,7 +251,7 @@
 
 
 def widen_kernel(rows, weight, after, wide):
-    taps, chans, chans_out = weight.shape
+    _, chans, chans_out = weight.shape
     span = rows + 2
     depth = span * chans
     for t in range(3):
@@ -262,7 +267,7 @@
 
 
 def widen_call(weight, after, rows):
-    taps, chans, chans_out = weight.shape
+    _, chans, chans_out = weight.shape
     vmem = pl.BlockSpec(memory_space=pltpu.VMEM)
     return pl.pallas_call(
         functools.partial(widen_kernel, rows),
@@ -276,10 +281,11 @@
 
 def conv_kernel(
     own, near, prev, prev_near, wide_v, bias,
-    out,
-    stack_v,
+    result,
+    stack_v, out, out_sem,
 ):
     frames, rows, cols, chans_out = out.shape
+    stores = []
     depth = wide_v.shape[1] // 3
     chans = depth // (rows + 2)
     half = lax.axis_index("cfg")
@@ -289,7 +295,7 @@
     first = half == 0
     band = 2 * rows * chans
     zero = jnp.zeros((chans, cols), BF16)
-    tail = frames * band
+    tail = frames * band + near.shape[0]
     for f in range(2 * frames):
         if f < frames:
             at = pl.ds(f * band, band)
@@ -320,6 +326,10 @@
         for y in range(rows):
             value = total[:, y * chans_out : (y + 1) * chans_out] + bias[...]
             out[f, y] = value.astype(BF16)
+            stores.append(pltpu.make_async_copy(out.at[f, y], result.at[f, y], out_sem.at[f * rows + y]))
+            stores[-1].start()
+    for copy in stores:
+        copy.wait()
 
 
 def conv_call(own, near, prev, prev_near, wide, bias, frames, rows):
@@ -331,8 +341,12 @@
         conv_kernel,
         out_shape=jax.ShapeDtypeStruct((frames, rows, cols, chans_out), BF16),
         in_specs=[vmem] * 6,
-        out_specs=vmem,
-        scratch_shapes=[pltpu.VMEM((2 * frames * depth, cols), BF16)],
+        out_specs=pl.BlockSpec(memory_space=pl.ANY),
+        scratch_shapes=[
+            pltpu.VMEM((2 * frames * depth, cols), BF16),
+            pltpu.VMEM((frames, rows, cols, chans_out), BF16),
+            pltpu.SemaphoreType.DMA((frames * rows,)),
+        ],
         compiler_params=limit(8),
         name="conv",
     )(own, near, prev, prev_near, wide, bias)
@@ -397,14 +411,13 @@
         prev = send(own, sizes, along)
         near = send(edge, sizes, lambda s, r, c: (s, 1 - r, c))
         prev_edge = send(edge, sizes, across)
-        prev, near, prev_edge = lax.optimization_barrier((prev, near, prev_edge))
-        prev = jnp.concatenate([prev, prev_edge], axis=0)
+        prev = jnp.concatenate([prev, near, prev_edge], axis=0)
         prev_near = send(prev, sizes, lambda s, r, c: (s, r, 1 - c))
     else:
         near = send(edge, sizes, lambda s, r, c: (s, r - 1, 1) if c == 0 else (s, r + 1, 0))
         prev = send(own, sizes, lambda s, r, c: (s + 1, r, c))
         prev_edge = send(edge, sizes, lambda s, r, c: (s + 1, r - 1, 1) if c == 0 else (s + 1, r + 1, 0))
-        prev = prev_near = jnp.concatenate([prev, prev_edge], axis=0)
+        prev = prev_near = jnp.concatenate([prev, near, prev_edge], axis=0)
     wide = widen_call(conv1_weight, edge, rows)
     return conv_call(own, near, prev, prev_near, wide, conv1_bias.reshape(1, -1), frames, rows)
 

time: 18.1 us -> 17.9 us (0.989)
  Pallas kernels: 7.27 us -> 7.03 us
  transfers between devices with their start and end apart: 5 -> 5, of which waited for: 3 -> 2; matrix products, arithmetic and copies ran while one was open for 0% -> 0% of each run, Pallas kernels for 0% -> 0%
where the time goes in v2:
time: 17.9 us; the launch traced here: 17.7 us
  Pallas kernels  7.03 us (39%)
  starting transfers between devices  5.17 us (29%)
  waiting for transfers between devices  4.15 us (23%)
  between operations  1.34 us (7%)
    pallas_call x1, Pallas kernels, head_call(): pl.pallas_call(head_kernel, out_shape=jax.ShapeDtypeStruct((frames * rows...  5.46 us
    ppermute x5, starting transfers between devices, send(): return lax.ppermute(value, RING, routes(sizes, rule))  5.17 us
    ppermute x5, waiting for transfers between devices, send(): return lax.ppermute(value, RING, routes(sizes, rule))  4.15 us
    pallas_call x1, Pallas kernels, conv_call(): pl.pallas_call(conv_kernel, out_shape=jax.ShapeDtypeStruct((frames, rows,...  1.39 us
  transfers between devices with their start and end apart: 5, of which 2 were waited for; matrix products, arithmetic and copies ran while one was open for 0% of the time, Pallas kernels for 0%

profile of v2, /device:TPU:0, one launch (start us, length us, event | category | flops | bytes accessed | tf_op | source)
XLA Modules:
  0.0 17.7 jit_solution(10391533794039478380)
XLA Ops:
  0.0 0.0 copy-start.1
  0.0 0.0 copy-start.2
  0.0 0.0 copy-start
  0.0 5.5 %head.1.mine = f32[192,128]{1,0:T(8,128)S(1)} custom-call(bf16[256,5120]{1,0:T(8,128)(2,1)} %bitcast.8, bf16[64,5120]{1,0:T(8,128)(2,1)} %bitcast.9, f32[2,5120]{1,0:T(2,128)} %mod.1, s32[1,256]{1,0:T(1,128)} %bitcast.10, f32[2,2,2048]{2,1,0:T(2,128)} %noisy.1, f32[1,16]{1,0:T(1,128)} %bitcast.11, f32[1,16]{1,0:T(1,128)} %bitcast.12, f32[16,16]{1,0:T(8,128)} %w2.1, ...), custom_call_target="tpu_custom_call" | custom-call | tf_op jit(solution)/shard_map/head/pallas_call | solution.py:179
  5.5 0.6 %collective-permute-start = (f32[192,128]{1,0:T(8,128)S(1)}, f32[192,128]{1,0:T(8,128)S(1)}, u32[]{:S(2)}, u32[]{:S(2)}) collective-permute-start(f32[192,128]{1,0:T(8,128)S(1)} %head.1.mine), channel_id=1, source_target_pairs={{0,1},{1,0},{2,3},{3,2},{4,5},{5,4},{6,7},{7,6},{8,9},{9,8},{10,11... | collective-permute-start | bytes 294920 | tf_op jit(solution)/shard_map/ppermute | solution.py:368
  7.3 0.0 collective-permute-done.theirs
  7.3 0.0 copy-done.1
  7.4 0.1 merge.1
  7.5 0.0 collective-permute-start.2
  7.5 3.9 %collective-permute-start.3 = (bf16[32,128]{1,0:T(8,128)(2,1)S(1)}, bf16[32,128]{1,0:T(8,128)(2,1)S(1)}, u32[]{:S(2)}, u32[]{:S(2)}) collective-permute-start(bf16[32,128]{1,0:T(8,128)(2,1)S(1)} %get-tuple-element.8.after), channel_id=1, source_target_pairs={{0,3},{1,7},{2,1},{3,5},{4,0},{5,11},{6,2},{7,9},{8,4},{9,15},{10,... | collective-permute-start | bytes 24584 | tf_op jit(solution)/shard_map/ppermute | solution.py:368
  11.4 0.5 %collective-permute-start.1 = (bf16[32,128]{1,0:T(8,128)(2,1)S(1)}, bf16[32,128]{1,0:T(8,128)(2,1)S(1)}, u32[]{:S(2)}, u32[]{:S(2)}) collective-permute-start(bf16[32,128]{1,0:T(8,128)(2,1)S(1)} %get-tuple-element.8.after), channel_id=1, source_target_pairs={{0,2},{1,3},{2,0},{3,1},{4,6},{5,7},{6,4},{7,5},{8,10},{9,11},{10,... | collective-permute-start | bytes 24584 | tf_op jit(solution)/shard_map/ppermute | solution.py:368
  11.9 0.0 collective-permute-done.2
  11.9 3.1 %collective-permute-done.1.near = bf16[32,128]{1,0:T(8,128)(2,1)S(1)} collective-permute-done((bf16[32,128]{1,0:T(8,128)(2,1)S(1)}, bf16[32,128]{1,0:T(8,128)(2,1)S(1)}, u32[]{:S(2)}, u32[]{:S(2)}) %collective-permute-start.1) | collective-permute-done | bytes 8224 | tf_op jit(solution)/shard_map/ppermute | solution.py:368
  15.0 0.0 collective-permute-done.3
  15.0 0.2 collective-permute-start.4
  15.2 0.0 copy-done.2
  15.2 0.0 copy-done
  15.2 0.1 widen.1.wide_v
  15.3 1.0 %collective-permute-done.4.prev_near = bf16[192,128]{1,0:T(8,128)(2,1)S(1)} collective-permute-done((bf16[192,128]{1,0:T(8,128)(2,1)S(1)}, bf16[192,128]{1,0:T(8,128)(2,1)S(1)}, u32[]{:S(2)}, u32[]{:S(2)}) %collective-permute-start.4) | collective-permute-done | bytes 49184 | tf_op jit(solution)/shard_map/ppermute | solution.py:368
  16.3 1.4 %conv.1 = bf16[2,2,128,384]{3,2,1,0:T(8,128)(2,1)} custom-call(bf16[128,128]{1,0:T(8,128)(2,1)S(1)} %get-tuple-element.7.own, bf16[32,128]{1,0:T(8,128)(2,1)S(1)} %collective-permute-done.1.near, bf16[192,128]{1,0:T(8,128)(2,1)S(1)} %constant_dynamic-update-slice_fusion.prev, bf16[192,128]{1,0:T(8,128)(2,1)S(1)} %collective-permute-done.4.prev_near, ...), custom_call_target="tpu_custom_call" | custom-call | tf_op jit(solution)/shard_map/conv/pallas_call | solution.py:340
  (4 shorter events, 0.0 us)
Async XLA Ops:
  0.0 7.3 %copy-start.1 = (s32[9]{0:T(128)S(1)}, s32[9]{0:T(128)}, u32[]{:S(2)}) copy-start(s32[9]{0:T(128)} %param.21) | copy-start | bytes 112
  0.0 15.2 %copy-start.2 = (f32[384]{0:T(512)S(1)}, f32[384]{0:T(512)}, u32[]{:S(2)}) copy-start(f32[384]{0:T(512)} %param.27) | copy-start | bytes 4612
  0.0 15.2 %copy-start = (bf16[27,16,384]{2,1,0:T(8,128)(2,1)S(1)}, bf16[27,16,384]{2,1,0:T(8,128)(2,1)}, u32[]{:S(2)}) copy-start(bf16[27,16,384]{2,1,0:T(8,128)(2,1)} %weight.1) | copy-start | bytes 995332
  5.5 1.9 %collective-permute-start = (f32[192,128]{1,0:T(8,128)S(1)}, f32[192,128]{1,0:T(8,128)S(1)}, u32[]{:S(2)}, u32[]{:S(2)}) collective-permute-start(f32[192,128]{1,0:T(8,128)S(1)} %head.1.mine), channel_id=1, source_target_pairs={{0,1},{1,0},{2,3},{3,2},{4,5},{5,4},{6,7},{7,6},{8,9},{9,8},{10,11... | collective-permute-start | bytes 294920 | tf_op jit(solution)/shard_map/ppermute | solution.py:368
  7.5 4.5 %collective-permute-start.2 = (bf16[128,128]{1,0:T(8,128)(2,1)S(1)}, bf16[128,128]{1,0:T(8,128)(2,1)S(1)}, u32[]{:S(2)}, u32[]{:S(2)}) collective-permute-start(bf16[128,128]{1,0:T(8,128)(2,1)S(1)} %get-tuple-element.7.own), channel_id=1, source_target_pairs={{0,1},{1,5},{2,3},{3,7},{4,0},{5,9},{6,2},{7,11},{8,4},{9,13},{10,... | collective-permute-start | bytes 98312 | tf_op jit(solution)/shard_map/ppermute | solution.py:368
  7.5 7.5 %collective-permute-start.3 = (bf16[32,128]{1,0:T(8,128)(2,1)S(1)}, bf16[32,128]{1,0:T(8,128)(2,1)S(1)}, u32[]{:S(2)}, u32[]{:S(2)}) collective-permute-start(bf16[32,128]{1,0:T(8,128)(2,1)S(1)} %get-tuple-element.8.after), channel_id=1, source_target_pairs={{0,3},{1,7},{2,1},{3,5},{4,0},{5,11},{6,2},{7,9},{8,4},{9,15},{10,... | collective-permute-start | bytes 24584 | tf_op jit(solution)/shard_map/ppermute | solution.py:368
  11.4 3.7 %collective-permute-start.1 = (bf16[32,128]{1,0:T(8,128)(2,1)S(1)}, bf16[32,128]{1,0:T(8,128)(2,1)S(1)}, u32[]{:S(2)}, u32[]{:S(2)}) collective-permute-start(bf16[32,128]{1,0:T(8,128)(2,1)S(1)} %get-tuple-element.8.after), channel_id=1, source_target_pairs={{0,2},{1,3},{2,0},{3,1},{4,6},{5,7},{6,4},{7,5},{8,10},{9,11},{10,... | collective-permute-start | bytes 24584 | tf_op jit(solution)/shard_map/ppermute | solution.py:368
  15.0 1.3 %collective-permute-start.4 = (bf16[192,128]{1,0:T(8,128)(2,1)S(1)}, bf16[192,128]{1,0:T(8,128)(2,1)S(1)}, u32[]{:S(2)}, u32[]{:S(2)}) collective-permute-start(bf16[192,128]{1,0:T(8,128)(2,1)S(1)} %constant_dynamic-update-slice_fusion.prev), channel_id=1, source_target_pairs={{0,1},{1,0},{2,3},{3,2},{4,5},{5,4},{6,7},{7,6},{8,9},{9,8},{10,11... | collective-permute-start | bytes 147464 | tf_op jit(solution)/shard_map/ppermute | solution.py:368

commit v3 on v2

--- a/solution.py
+++ b/solution.py
@@ -23,6 +23,14 @@
 
 def iota(shape, dim):
     return lax.broadcasted_iota(jnp.int32, shape, dim)
+
+
+def split(value, terms):
+    parts = []
+    for _ in range(terms):
+        parts.append(value.astype(BF16))
+        value = value - parts[-1].astype(F32)
+    return parts
 
 
 def head_kernel(
@@ -99,6 +107,8 @@
     spot_j = iota((outs, outs), 1) // chans
     match = (spot_o % 2 == spot_j // 2) & (spot_o // 2 == spot_j % 2)
     mixer = jnp.where(match, jnp.concatenate([mix[:, :outs]] * blocks, axis=0), 0.0)
+    high, low = split(mixer, 2)
+    mixer = jnp.concatenate([high, high, low], axis=1)
 
     for copy in big:
         copy.wait()
@@ -124,6 +134,7 @@
 
     group = 32
     total = jnp.zeros((wcat_v.shape[0], tokens), F32)
+    pivot_row = None
     for k in range(chunks):
         loads[k].wait()
         for copy in loads[5:] if k == 0 else ():
@@ -145,21 +156,21 @@
                 gap = values[:, j : j + lanes] - pivot
                 squares = squares + gap * gap
             square_v[rows, :] = squares
-
-    square = mm(jnp.ones((8, lanes), F32), square_v[...], NT, HIGHEST)[0:1] * (1.0 / width)
-    pivot = mm(jnp.ones((8, lanes), F32), pivot_v[...], NT, HIGHEST)[0:1] * (1.0 / lanes)
+        if k == 0:
+            parts = jnp.concatenate(split(pivot_v[...], 3), axis=1)
+            pivot_row = mm(jnp.ones((16, 3 * lanes), BF16), parts, NT)[0:1] * (1.0 / lanes)
+
+    parts = jnp.concatenate(split(square_v[...], 3), axis=1)
+    square = mm(jnp.ones((16, 3 * lanes), BF16), parts, NT)[0:1] * (1.0 / width)
     center = total[2 * outs : 2 * outs + 1] * (1.0 / width)
-    gap = center - pivot
+    gap = center - pivot_row
     inverse = lax.rsqrt(jnp.maximum(square - gap * gap, 0.0) + 1e-06)
     head = (total[0:outs] + total[outs : 2 * outs] - center * col_sum) * inverse + shift_sum
-    mixed = mm(mixer, head, NN, HIGHEST)
+    high, low = split(head, 2)
+    mixed = mm(mixer, jnp.concatenate([high, low, high], axis=0))
     side = outs // 2
     mixed = jnp.concatenate([mixed[:side], mixed[side:]], axis=1)
-    high = mixed.astype(BF16)
-    rest = mixed - high.astype(F32)
-    middle = rest.astype(BF16)
-    low = (rest - middle.astype(F32)).astype(BF16)
-    placed = mm(jnp.concatenate([high, middle, low], axis=0), place_v[...], NT)
+    placed = mm(jnp.concatenate(split(mixed, 3), axis=0), place_v[...], NT)
     placed = placed[:side] + placed[side : 2 * side] + placed[2 * side :]
     for f in range(frames):
         for i in range(token_rows):
@@ -250,106 +261,149 @@
     return pltpu.CompilerParams(vmem_limit_bytes=mebibytes * 2**20)
 
 
-def widen_kernel(rows, weight, after, wide):
+def widen_kernel(rows, weight, after, early, late):
     _, chans, chans_out = weight.shape
     span = rows + 2
-    depth = span * chans
-    for t in range(3):
+    for wide, base in ((early, 0), (late, 1)):
         for w in range(3):
-            for y in range(rows):
+            for t in range(2):
                 for q in range(span):
-                    u = q - y
-                    if 0 <= u < 3:
-                        value = weight[9 * t + 3 * u + w]
-                    else:
-                        value = jnp.zeros((chans, chans_out), BF16)
-                    wide[w, pl.ds(t * depth + q * chans, chans), pl.ds(y * chans_out, chans_out)] = value
+                    at = pl.ds(((w * 2 + t) * span + q) * chans, chans)
+                    for y in range(rows):
+                        u = q - y
+                        if 0 <= u < 3:
+                            value = weight[9 * (t + base) + 3 * u + w]
+                        else:
+                            value = jnp.zeros((chans, chans_out), BF16)
+                        wide[at, pl.ds(y * chans_out, chans_out)] = value
 
 
 def widen_call(weight, after, rows):
     _, chans, chans_out = weight.shape
     vmem = pl.BlockSpec(memory_space=pltpu.VMEM)
+    wide = jax.ShapeDtypeStruct((6 * (rows + 2) * chans, rows * chans_out), BF16)
     return pl.pallas_call(
         functools.partial(widen_kernel, rows),
-        out_shape=jax.ShapeDtypeStruct((3, 3 * (rows + 2) * chans, rows * chans_out), BF16),
+        out_shape=(wide, wide),
         in_specs=[vmem, pl.BlockSpec(memory_space=pl.ANY)],
-        out_specs=vmem,
+        out_specs=(vmem, vmem),
         compiler_params=limit(8),
         name="widen",
     )(weight, after)
 
 
-def conv_kernel(
-    own, near, prev, prev_near, wide_v, bias,
-    result,
-    stack_v, out, out_sem,
-):
+def columns(stack_v):
+    cols = stack_v.shape[1]
+    picks = [iota((cols, cols), 0) + (w - 1) == iota((cols, cols), 1) for w in range(3)]
+    pick = jnp.concatenate([jnp.where(hit, 1.0, 0.0).astype(BF16) for hit in picks], axis=0)
+    moved = mm(pick, stack_v[...], NT).astype(BF16)
+    depth = moved.shape[1] // 2
+    sides = []
+    for f in range(2):
+        pieces = [moved[w * cols : (w + 1) * cols, f * depth : (f + 1) * depth] for w in range(3)]
+        sides.append(jnp.concatenate(pieces, axis=1))
+    return sides
+
+
+def late_kernel(rows, own, near, wide, bias, total, stack_v):
+    chans = near.shape[0] // 2
+    band = own.shape[0] // 2
+    row = lax.axis_index("rows")
+    first = lax.axis_index("cfg") == 0
+    inner = jnp.where(first, row > 0, row < lax.axis_size("rows") - 1)
+    depth = stack_v.shape[0] // 4
+    frames = []
+    for f in range(2):
+        edge = near[pl.ds(f * chans, chans), :]
+        edge = jnp.where(inner, edge, jnp.zeros_like(edge))
+        trim = band - (depth - chans)
+        base = own[pl.ds(f * band, band), :]
+        frames.append(
+            jnp.where(
+                first,
+                jnp.concatenate([edge, base[: band - trim]], axis=0),
+                jnp.concatenate([base[trim:], edge], axis=0),
+            )
+        )
+    stack_v[0:depth, :] = jnp.zeros((depth, stack_v.shape[1]), BF16)
+    stack_v[depth : 2 * depth, :] = frames[0]
+    stack_v[2 * depth : 3 * depth, :] = frames[0]
+    stack_v[3 * depth :, :] = frames[1]
+    for f, side in enumerate(columns(stack_v)):
+        total[f] = mm(side, wide[...]) + jnp.concatenate([bias[...]] * rows, axis=1)
+
+
+def late_call(own, near, wide, bias, rows):
+    cols = own.shape[1]
+    depth = wide.shape[0] // 6
+    vmem = pl.BlockSpec(memory_space=pltpu.VMEM)
+    return pl.pallas_call(
+        functools.partial(late_kernel, rows),
+        out_shape=jax.ShapeDtypeStruct((2, cols, wide.shape[1]), F32),
+        in_specs=[vmem] * 4,
+        out_specs=vmem,
+        scratch_shapes=[pltpu.VMEM((4 * depth, cols), BF16)],
+        compiler_params=limit(8),
+        name="late",
+    )(own, near, wide, bias)
+
+
+def early_kernel(prev, prev_near, wide, total, result, stack_v, out, out_sem):
     frames, rows, cols, chans_out = out.shape
+    depth = stack_v.shape[0] // 4
+    chans = depth // (rows + 2)
+    band = 2 * rows * chans
+    tail = prev.shape[0] - frames * chans
+    row = lax.axis_index("rows")
+    first = lax.axis_index("cfg") == 0
+    past = lax.axis_index("seq") > 0
+    inner = jnp.where(first, row > 0, row < lax.axis_size("rows") - 1)
+    trim = band - (depth - chans)
+    for f in range(frames):
+        at = pl.ds(f * band, band)
+        base = jnp.where(first, prev_near[at, :], prev[at, :])
+        base = jnp.where(past, base, jnp.zeros_like(base))
+        at = pl.ds(tail + f * chans, chans)
+        edge = jnp.where(first, prev_near[at, :], prev[at, :])
+        edge = jnp.where(past & inner, edge, jnp.zeros_like(edge))
+        value = jnp.where(
+            first,
+            jnp.concatenate([edge, base[: band - trim]], axis=0),
+            jnp.concatenate([base[trim:], edge], axis=0),
+        )
+        stack_v[f * depth : (f + 1) * depth, :] = value
+        if f == 1:
+            stack_v[2 * depth : 3 * depth, :] = value
+    stack_v[3 * depth :, :] = jnp.zeros((depth, cols), BF16)
     stores = []
-    depth = wide_v.shape[1] // 3
-    chans = depth // (rows + 2)
-    half = lax.axis_index("cfg")
-    row = lax.axis_index("rows")
-    past = lax.axis_index("seq") > 0
-    inner = jnp.where(half == 0, row > 0, row < lax.axis_size("rows") - 1)
-    first = half == 0
-    band = 2 * rows * chans
-    zero = jnp.zeros((chans, cols), BF16)
-    tail = frames * band + near.shape[0]
-    for f in range(2 * frames):
-        if f < frames:
-            at = pl.ds(f * band, band)
-            base = jnp.where(first, prev_near[at, :], prev[at, :])
-            base = jnp.where(past, base, jnp.zeros_like(base))
-            at = pl.ds(tail + f * chans, chans)
-            edge = jnp.where(first, prev_near[at, :], prev[at, :])
-            edge = jnp.where(past & inner, edge, zero)
-        else:
-            base = own[pl.ds((f - frames) * band, band), :]
-            edge = jnp.where(inner, near[pl.ds((f - frames) * chans, chans), :], zero)
-        keep = (rows + 1) * chans
-        stack_v[pl.ds(f * depth, depth), :] = jnp.where(
-            first,
-            jnp.concatenate([edge, base[:keep]], axis=0),
-            jnp.concatenate([base[band - keep :], edge], axis=0),
-        )
-    latents = stack_v[...]
-    shifted = []
-    for w in range(3):
-        pick = (iota((cols, cols), 0) + (w - 1) == iota((cols, cols), 1)).astype(F32).astype(BF16)
-        shifted.append(mm(pick, latents, NT).astype(BF16))
-    for f in range(frames):
-        window = slice(f * depth, (f + 3) * depth)
-        total = mm(shifted[0][:, window], wide_v[0])
-        for w in range(1, 3):
-            total = total + mm(shifted[w][:, window], wide_v[w])
+    for f, side in enumerate(columns(stack_v)):
         for y in range(rows):
-            value = total[:, y * chans_out : (y + 1) * chans_out] + bias[...]
-            out[f, y] = value.astype(BF16)
+            span = pl.ds(y * chans_out, chans_out)
+            out[f, y] = (mm(side, wide[:, span]) + total[f, :, span]).astype(BF16)
             stores.append(pltpu.make_async_copy(out.at[f, y], result.at[f, y], out_sem.at[f * rows + y]))
             stores[-1].start()
     for copy in stores:
         copy.wait()
 
 
-def conv_call(own, near, prev, prev_near, wide, bias, frames, rows):
-    cols = own.shape[1]
-    depth = wide.shape[1] // 3
-    chans_out = wide.shape[2] // rows
+def early_call(prev, prev_near, wide, total, rows):
+    frames, cols, _ = total.shape
+    depth = wide.shape[0] // 6
+    chans_out = wide.shape[1] // rows
     vmem = pl.BlockSpec(memory_space=pltpu.VMEM)
     return pl.pallas_call(
-        conv_kernel,
+        early_kernel,
         out_shape=jax.ShapeDtypeStruct((frames, rows, cols, chans_out), BF16),
-        in_specs=[vmem] * 6,
+        in_specs=[vmem] * 4,
         out_specs=pl.BlockSpec(memory_space=pl.ANY),
         scratch_shapes=[
-            pltpu.VMEM((2 * frames * depth, cols), BF16),
+            pltpu.VMEM((4 * depth, cols), BF16),
             pltpu.VMEM((frames, rows, cols, chans_out), BF16),
             pltpu.SemaphoreType.DMA((frames * rows,)),
         ],
         compiler_params=limit(8),
-        name="conv",
-    )(own, near, prev, prev_near, wide, bias)
+        name="early",
+    )(prev, prev_near, wide, total)
 
 
 def routes(sizes, rule):
@@ -418,8 +472,9 @@
         prev = send(own, sizes, lambda s, r, c: (s + 1, r, c))
         prev_edge = send(edge, sizes, lambda s, r, c: (s + 1, r - 1, 1) if c == 0 else (s + 1, r + 1, 0))
         prev = prev_near = jnp.concatenate([prev, near, prev_edge], axis=0)
-    wide = widen_call(conv1_weight, edge, rows)
-    return conv_call(own, near, prev, prev_near, wide, conv1_bias.reshape(1, -1), frames, rows)
+    early, late = widen_call(conv1_weight, edge, rows)
+    total = late_call(own, near, late, conv1_bias.reshape(1, -1), rows)
+    return early_call(prev, prev_near, early, total, rows)
 
 
 def solution(mesh):

time: 17.9 us -> 16.8 us (0.939)
  the two profiles are of different devices: /device:TPU:0 before, /device:TPU:1 now
where the time goes in v3:
time: 16.8 us; the launch traced here: 16.5 us
  Pallas kernels  7.45 us (44%)
  starting transfers between devices  5.42 us (32%)
  waiting for transfers between devices  2.23 us (13%)
  between operations  1.35 us (8%)
    ppermute x5, starting transfers between devices, send(): return lax.ppermute(value, RING, routes(sizes, rule))  5.42 us
    pallas_call x1, Pallas kernels, head_call(): pl.pallas_call(head_kernel, out_shape=jax.ShapeDtypeStruct((frames * rows...  5.34 us
    ppermute x5, waiting for transfers between devices, send(): return lax.ppermute(value, RING, routes(sizes, rule))  2.23 us
    pallas_call x1, Pallas kernels, early_call(): pl.pallas_call(early_kernel, out_shape=jax.ShapeDtypeStruct((frames, rows...  1.3 us
    pallas_call x1, Pallas kernels, late_call(): pl.pallas_call(functools.partial(late_kernel, rows), out_shape=jax.ShapeD...  0.61 us
  transfers between devices with their start and end apart: 5, of which 2 were waited for; matrix products, arithmetic and copies ran while one was open for 0% of the time, Pallas kernels for 4%

profile of v3, /device:TPU:1, one launch (start us, length us, event | category | flops | bytes accessed | tf_op | source)
XLA Modules:
  0.0 16.5 jit_solution(17167086660135863163)
XLA Ops:
  0.0 0.0 copy-start.1
  0.0 0.0 copy-start.2
  0.0 0.0 copy-start
  0.0 5.3 %head.1.mine = f32[192,128]{1,0:T(8,128)S(1)} custom-call(bf16[256,5120]{1,0:T(8,128)(2,1)} %bitcast.8, bf16[64,5120]{1,0:T(8,128)(2,1)} %bitcast.9, f32[2,5120]{1,0:T(2,128)} %mod.1, s32[1,256]{1,0:T(1,128)} %bitcast.10, f32[2,2,2048]{2,1,0:T(2,128)} %noisy.1, f32[1,16]{1,0:T(1,128)} %bitcast.11, f32[1,16]{1,0:T(1,128)} %bitcast.12, f32[16,16]{1,0:T(8,128)} %w2.1, ...), custom_call_target="tpu_custom_call" | custom-call | tf_op jit(solution)/shard_map/head/pallas_call | solution.py:190
  5.4 0.1 collective-permute-start
  6.7 0.0 collective-permute-done.theirs
  6.7 0.0 copy-done.1
  6.8 0.1 merge.1
  6.9 2.8 %collective-permute-start.1 = (bf16[128,128]{1,0:T(8,128)(2,1)S(1)}, bf16[128,128]{1,0:T(8,128)(2,1)S(1)}, u32[]{:S(2)}, u32[]{:S(2)}) collective-permute-start(bf16[128,128]{1,0:T(8,128)(2,1)S(1)} %get-tuple-element.9.own), channel_id=1, source_target_pairs={{0,1},{1,5},{2,3},{3,7},{4,0},{5,9},{6,2},{7,11},{8,4},{9,13},{10,... | collective-permute-start | bytes 98312 | tf_op jit(solution)/shard_map/ppermute | solution.py:422
  9.7 1.2 %collective-permute-start.2 = (bf16[32,128]{1,0:T(8,128)(2,1)S(1)}, bf16[32,128]{1,0:T(8,128)(2,1)S(1)}, u32[]{:S(2)}, u32[]{:S(2)}) collective-permute-start(bf16[32,128]{1,0:T(8,128)(2,1)S(1)} %get-tuple-element.10.after), channel_id=1, source_target_pairs={{0,2},{1,3},{2,0},{3,1},{4,6},{5,7},{6,4},{7,5},{8,10},{9,11},{10,... | collective-permute-start | bytes 24584 | tf_op jit(solution)/shard_map/ppermute | solution.py:422
  10.9 1.3 %collective-permute-start.3 = (bf16[32,128]{1,0:T(8,128)(2,1)S(1)}, bf16[32,128]{1,0:T(8,128)(2,1)S(1)}, u32[]{:S(2)}, u32[]{:S(2)}) collective-permute-start(bf16[32,128]{1,0:T(8,128)(2,1)S(1)} %get-tuple-element.10.after), channel_id=1, source_target_pairs={{0,3},{1,7},{2,1},{3,5},{4,0},{5,11},{6,2},{7,9},{8,4},{9,15},{10,... | collective-permute-start | bytes 24584 | tf_op jit(solution)/shard_map/ppermute | solution.py:422
  12.1 0.0 collective-permute-done.1
  12.1 0.0 collective-permute-done.2.near
  12.2 1.8 %collective-permute-done.3 = bf16[32,128]{1,0:T(8,128)(2,1)S(1)} collective-permute-done((bf16[32,128]{1,0:T(8,128)(2,1)S(1)}, bf16[32,128]{1,0:T(8,128)(2,1)S(1)}, u32[]{:S(2)}, u32[]{:S(2)}) %collective-permute-start.3) | collective-permute-done | bytes 8224 | tf_op jit(solution)/shard_map/ppermute | solution.py:422
  14.0 0.1 collective-permute-start.4
  14.0 0.0 copy-done.2
  14.0 0.0 copy-done
  14.0 0.1 widen.1
  14.1 0.6 %late.1.total = f32[2,128,768]{2,1,0:T(8,128)S(1)} custom-call(bf16[128,128]{1,0:T(8,128)(2,1)S(1)} %get-tuple-element.9.own, bf16[32,128]{1,0:T(8,128)(2,1)S(1)} %collective-permute-done.2.near, bf16[384,768]{1,0:T(8,128)(2,1)S(1)} %get-tuple-element.12.wide, f32[1,384]{1,0:T(1,128)S(1)} %reshape.27.bias), custom_call_target="tpu_custom_call" | custom-call | tf_op jit(solution)/shard_map/late/pallas_call | solution.py:340
  14.8 0.4 %collective-permute-done.4.prev_near = bf16[192,128]{1,0:T(8,128)(2,1)S(1)} collective-permute-done((bf16[192,128]{1,0:T(8,128)(2,1)S(1)}, bf16[192,128]{1,0:T(8,128)(2,1)S(1)}, u32[]{:S(2)}, u32[]{:S(2)}) %collective-permute-start.4) | collective-permute-done | bytes 49184 | tf_op jit(solution)/shard_map/ppermute | solution.py:422
  15.2 1.3 %early.1 = bf16[2,2,128,384]{3,2,1,0:T(8,128)(2,1)} custom-call(bf16[192,128]{1,0:T(8,128)(2,1)S(1)} %constant_dynamic-update-slice_fusion.prev, bf16[192,128]{1,0:T(8,128)(2,1)S(1)} %collective-permute-done.4.prev_near, bf16[384,768]{1,0:T(8,128)(2,1)S(1)} %get-tuple-element.11.wide, f32[2,128,768]{2,1,0:T(8,128)S(1)} %late.1.total), custom_call_target="tpu_custom_call" | custom-call | tf_op jit(solution)/shard_map/early/pallas_call | solution.py:394
  (4 shorter events, 0.0 us)
Async XLA Ops:
  0.0 6.7 %copy-start.1 = (s32[9]{0:T(128)S(1)}, s32[9]{0:T(128)}, u32[]{:S(2)}) copy-start(s32[9]{0:T(128)} %param.21) | copy-start | bytes 112
  0.0 14.0 %copy-start.2 = (f32[384]{0:T(512)S(1)}, f32[384]{0:T(512)}, u32[]{:S(2)}) copy-start(f32[384]{0:T(512)} %param.27) | copy-start | bytes 4612
  0.0 14.0 %copy-start = (bf16[27,16,384]{2,1,0:T(8,128)(2,1)S(1)}, bf16[27,16,384]{2,1,0:T(8,128)(2,1)}, u32[]{:S(2)}) copy-start(bf16[27,16,384]{2,1,0:T(8,128)(2,1)} %weight.1) | copy-start | bytes 995332
  5.4 1.4 %collective-permute-start = (f32[192,128]{1,0:T(8,128)S(1)}, f32[192,128]{1,0:T(8,128)S(1)}, u32[]{:S(2)}, u32[]{:S(2)}) collective-permute-start(f32[192,128]{1,0:T(8,128)S(1)} %head.1.mine), channel_id=1, source_target_pairs={{0,1},{1,0},{2,3},{3,2},{4,5},{5,4},{6,7},{7,6},{8,9},{9,8},{10,11... | collective-permute-start | bytes 294920 | tf_op jit(solution)/shard_map/ppermute | solution.py:422
  6.9 5.3 %collective-permute-start.1 = (bf16[128,128]{1,0:T(8,128)(2,1)S(1)}, bf16[128,128]{1,0:T(8,128)(2,1)S(1)}, u32[]{:S(2)}, u32[]{:S(2)}) collective-permute-start(bf16[128,128]{1,0:T(8,128)(2,1)S(1)} %get-tuple-element.9.own), channel_id=1, source_target_pairs={{0,1},{1,5},{2,3},{3,7},{4,0},{5,9},{6,2},{7,11},{8,4},{9,13},{10,... | collective-permute-start | bytes 98312 | tf_op jit(solution)/shard_map/ppermute | solution.py:422
  9.7 2.5 %collective-permute-start.2 = (bf16[32,128]{1,0:T(8,128)(2,1)S(1)}, bf16[32,128]{1,0:T(8,128)(2,1)S(1)}, u32[]{:S(2)}, u32[]{:S(2)}) collective-permute-start(bf16[32,128]{1,0:T(8,128)(2,1)S(1)} %get-tuple-element.10.after), channel_id=1, source_target_pairs={{0,2},{1,3},{2,0},{3,1},{4,6},{5,7},{6,4},{7,5},{8,10},{9,11},{10,... | collective-permute-start | bytes 24584 | tf_op jit(solution)/shard_map/ppermute | solution.py:422
  10.9 3.1 %collective-permute-start.3 = (bf16[32,128]{1,0:T(8,128)(2,1)S(1)}, bf16[32,128]{1,0:T(8,128)(2,1)S(1)}, u32[]{:S(2)}, u32[]{:S(2)}) collective-permute-start(bf16[32,128]{1,0:T(8,128)(2,1)S(1)} %get-tuple-element.10.after), channel_id=1, source_target_pairs={{0,3},{1,7},{2,1},{3,5},{4,0},{5,11},{6,2},{7,9},{8,4},{9,15},{10,... | collective-permute-start | bytes 24584 | tf_op jit(solution)/shard_map/ppermute | solution.py:422
  14.0 1.2 %collective-permute-start.4 = (bf16[192,128]{1,0:T(8,128)(2,1)S(1)}, bf16[192,128]{1,0:T(8,128)(2,1)S(1)}, u32[]{:S(2)}, u32[]{:S(2)}) collective-permute-start(bf16[192,128]{1,0:T(8,128)(2,1)S(1)} %constant_dynamic-update-slice_fusion.prev), channel_id=1, source_target_pairs={{0,1},{1,0},{2,3},{3,2},{4,5},{5,4},{6,7},{7,6},{8,9},{9,8},{10,11... | collective-permute-start | bytes 147464 | tf_op jit(solution)/shard_map/ppermute | solution.py:422

commit v4 on v3

--- a/solution.py
+++ b/solution.py
@@ -112,7 +112,7 @@
 
     for copy in big:
         copy.wait()
-    for copy in loads[1:5]:
+    for copy in loads[1:1]:
         copy.start()
     piece = 512
     col_sum = jnp.zeros((outs, lanes), F32)
@@ -132,15 +132,14 @@
     col_sum = jnp.sum(col_sum, axis=1, keepdims=True)
     shift_sum = jnp.sum(shift_sum, axis=1, keepdims=True)
 
-    group = 32
+    group = 16
     total = jnp.zeros((wcat_v.shape[0], tokens), F32)
     pivot_row = None
     for k in range(chunks):
         loads[k].wait()
-        for copy in loads[5:] if k == 0 else ():
+        for copy in ():
             copy.start()
         span = pl.ds(k * chunk, chunk)
-        total = total + mm(wcat_v[:, span], x_v[:, span], NT)
         for g in range(0, tokens, group):
             rows = pl.ds(g, group)
             values = x_v[rows, span].astype(F32)
@@ -156,6 +155,7 @@
                 gap = values[:, j : j + lanes] - pivot
                 squares = squares + gap * gap
             square_v[rows, :] = squares
+        total = total + mm(wcat_v[:, span], x_v[:, span], NT)
         if k == 0:
             parts = jnp.concatenate(split(pivot_v[...], 3), axis=1)
             pivot_row = mm(jnp.ones((16, 3 * lanes), BF16), parts, NT)[0:1] * (1.0 / lanes)
@@ -184,7 +184,7 @@
     chans = w2.shape[0]
     frames, rows, row_lanes = noisy.shape
     cols = row_lanes // chans
-    chunks = 5
+    chunks = 1
     hbm = pl.BlockSpec(memory_space=pl.ANY)
     vmem = pltpu.VMEM
     return pl.pallas_call(

time: 16.8 us -> 16 us (0.952)
  Pallas kernels: 7.45 us -> 6.67 us
    pallas_call x1, Pallas kernels: 5.34 us -> 4.55 us  [head_call(): pl.pallas_call(head_kernel, out_shape=jax.ShapeDtypeStruct((frames * rows...]
  transfers between devices with their start and end apart: 5 -> 5, of which waited for: 2 -> 2; matrix products, arithmetic and copies ran while one was open for 0% -> 0% of each run, Pallas kernels for 4% -> 5%
where the time goes in v4:
time: 16 us; the launch traced here: 15.7 us
  Pallas kernels  6.67 us (42%)
  starting transfers between devices  5.42 us (34%)
  waiting for transfers between devices  2.23 us (14%)
  between operations  1.35 us (8%)
    ppermute x5, starting transfers between devices, send(): return lax.ppermute(value, RING, routes(sizes, rule))  5.42 us
    pallas_call x1, Pallas kernels, head_call(): pl.pallas_call(head_kernel, out_shape=jax.ShapeDtypeStruct((frames * rows...  4.55 us
    ppermute x5, waiting for transfers between devices, send(): return lax.ppermute(value, RING, routes(sizes, rule))  2.23 us
    pallas_call x1, Pallas kernels, early_call(): pl.pallas_call(early_kernel, out_shape=jax.ShapeDtypeStruct((frames, rows...  1.3 us
    pallas_call x1, Pallas kernels, late_call(): pl.pallas_call(functools.partial(late_kernel, rows), out_shape=jax.ShapeD...  0.61 us
  transfers between devices with their start and end apart: 5, of which 2 were waited for; matrix products, arithmetic and copies ran while one was open for 0% of the time, Pallas kernels for 5%

profile of v4, /device:TPU:1, one launch (start us, length us, event | category | flops | bytes accessed | tf_op | source)
XLA Modules:
  0.0 15.7 jit_solution(9356223911478311394)
XLA Ops:
  0.0 0.0 copy-start.1
  0.0 0.0 copy-start.2
  0.0 0.0 copy-start
  0.0 4.6 %head.1.mine = f32[192,128]{1,0:T(8,128)S(1)} custom-call(bf16[256,5120]{1,0:T(8,128)(2,1)} %bitcast.8, bf16[64,5120]{1,0:T(8,128)(2,1)} %bitcast.9, f32[2,5120]{1,0:T(2,128)} %mod.1, s32[1,256]{1,0:T(1,128)} %bitcast.10, f32[2,2,2048]{2,1,0:T(2,128)} %noisy.1, f32[1,16]{1,0:T(1,128)} %bitcast.11, f32[1,16]{1,0:T(1,128)} %bitcast.12, f32[16,16]{1,0:T(8,128)} %w2.1, ...), custom_call_target="tpu_custom_call" | custom-call | tf_op jit(solution)/shard_map/head/pallas_call | solution.py:190
  4.6 0.1 collective-permute-start
  6.0 0.0 collective-permute-done.theirs
  6.0 0.0 copy-done.1
  6.0 0.1 merge.1
  6.1 2.8 %collective-permute-start.1 = (bf16[128,128]{1,0:T(8,128)(2,1)S(1)}, bf16[128,128]{1,0:T(8,128)(2,1)S(1)}, u32[]{:S(2)}, u32[]{:S(2)}) collective-permute-start(bf16[128,128]{1,0:T(8,128)(2,1)S(1)} %get-tuple-element.9.own), channel_id=1, source_target_pairs={{0,1},{1,5},{2,3},{3,7},{4,0},{5,9},{6,2},{7,11},{8,4},{9,13},{10,... | collective-permute-start | bytes 98312 | tf_op jit(solution)/shard_map/ppermute | solution.py:422
  8.9 1.2 %collective-permute-start.2 = (bf16[32,128]{1,0:T(8,128)(2,1)S(1)}, bf16[32,128]{1,0:T(8,128)(2,1)S(1)}, u32[]{:S(2)}, u32[]{:S(2)}) collective-permute-start(bf16[32,128]{1,0:T(8,128)(2,1)S(1)} %get-tuple-element.10.after), channel_id=1, source_target_pairs={{0,2},{1,3},{2,0},{3,1},{4,6},{5,7},{6,4},{7,5},{8,10},{9,11},{10,... | collective-permute-start | bytes 24584 | tf_op jit(solution)/shard_map/ppermute | solution.py:422
  10.1 1.3 %collective-permute-start.3 = (bf16[32,128]{1,0:T(8,128)(2,1)S(1)}, bf16[32,128]{1,0:T(8,128)(2,1)S(1)}, u32[]{:S(2)}, u32[]{:S(2)}) collective-permute-start(bf16[32,128]{1,0:T(8,128)(2,1)S(1)} %get-tuple-element.10.after), channel_id=1, source_target_pairs={{0,3},{1,7},{2,1},{3,5},{4,0},{5,11},{6,2},{7,9},{8,4},{9,15},{10,... | collective-permute-start | bytes 24584 | tf_op jit(solution)/shard_map/ppermute | solution.py:422
  11.4 0.0 collective-permute-done.1
  11.4 0.0 collective-permute-done.2.near
  11.4 1.8 %collective-permute-done.3 = bf16[32,128]{1,0:T(8,128)(2,1)S(1)} collective-permute-done((bf16[32,128]{1,0:T(8,128)(2,1)S(1)}, bf16[32,128]{1,0:T(8,128)(2,1)S(1)}, u32[]{:S(2)}, u32[]{:S(2)}) %collective-permute-start.3) | collective-permute-done | bytes 8224 | tf_op jit(solution)/shard_map/ppermute | solution.py:422
  13.2 0.1 collective-permute-start.4
  13.2 0.0 copy-done.2
  13.2 0.0 copy-done
  13.3 0.1 widen.1
  13.4 0.6 %late.1.total = f32[2,128,768]{2,1,0:T(8,128)S(1)} custom-call(bf16[128,128]{1,0:T(8,128)(2,1)S(1)} %get-tuple-element.9.own, bf16[32,128]{1,0:T(8,128)(2,1)S(1)} %collective-permute-done.2.near, bf16[384,768]{1,0:T(8,128)(2,1)S(1)} %get-tuple-element.12.wide, f32[1,384]{1,0:T(1,128)S(1)} %reshape.27.bias), custom_call_target="tpu_custom_call" | custom-call | tf_op jit(solution)/shard_map/late/pallas_call | solution.py:340
  14.0 0.4 %collective-permute-done.4.prev_near = bf16[192,128]{1,0:T(8,128)(2,1)S(1)} collective-permute-done((bf16[192,128]{1,0:T(8,128)(2,1)S(1)}, bf16[192,128]{1,0:T(8,128)(2,1)S(1)}, u32[]{:S(2)}, u32[]{:S(2)}) %collective-permute-start.4) | collective-permute-done | bytes 49184 | tf_op jit(solution)/shard_map/ppermute | solution.py:422
  14.4 1.3 %early.1 = bf16[2,2,128,384]{3,2,1,0:T(8,128)(2,1)} custom-call(bf16[192,128]{1,0:T(8,128)(2,1)S(1)} %constant_dynamic-update-slice_fusion.prev, bf16[192,128]{1,0:T(8,128)(2,1)S(1)} %collective-permute-done.4.prev_near, bf16[384,768]{1,0:T(8,128)(2,1)S(1)} %get-tuple-element.11.wide, f32[2,128,768]{2,1,0:T(8,128)S(1)} %late.1.total), custom_call_target="tpu_custom_call" | custom-call | tf_op jit(solution)/shard_map/early/pallas_call | solution.py:394
  (4 shorter events, 0.0 us)
Async XLA Ops:
  0.0 6.0 %copy-start.1 = (s32[9]{0:T(128)S(1)}, s32[9]{0:T(128)}, u32[]{:S(2)}) copy-start(s32[9]{0:T(128)} %param.21) | copy-start | bytes 112
  0.0 13.2 %copy-start.2 = (f32[384]{0:T(512)S(1)}, f32[384]{0:T(512)}, u32[]{:S(2)}) copy-start(f32[384]{0:T(512)} %param.27) | copy-start | bytes 4612
  0.0 13.2 %copy-start = (bf16[27,16,384]{2,1,0:T(8,128)(2,1)S(1)}, bf16[27,16,384]{2,1,0:T(8,128)(2,1)}, u32[]{:S(2)}) copy-start(bf16[27,16,384]{2,1,0:T(8,128)(2,1)} %weight.1) | copy-start | bytes 995332
  4.6 1.4 %collective-permute-start = (f32[192,128]{1,0:T(8,128)S(1)}, f32[192,128]{1,0:T(8,128)S(1)}, u32[]{:S(2)}, u32[]{:S(2)}) collective-permute-start(f32[192,128]{1,0:T(8,128)S(1)} %head.1.mine), channel_id=1, source_target_pairs={{0,1},{1,0},{2,3},{3,2},{4,5},{5,4},{6,7},{7,6},{8,9},{9,8},{10,11... | collective-permute-start | bytes 294920 | tf_op jit(solution)/shard_map/ppermute | solution.py:422
  6.1 5.3 %collective-permute-start.1 = (bf16[128,128]{1,0:T(8,128)(2,1)S(1)}, bf16[128,128]{1,0:T(8,128)(2,1)S(1)}, u32[]{:S(2)}, u32[]{:S(2)}) collective-permute-start(bf16[128,128]{1,0:T(8,128)(2,1)S(1)} %get-tuple-element.9.own), channel_id=1, source_target_pairs={{0,1},{1,5},{2,3},{3,7},{4,0},{5,9},{6,2},{7,11},{8,4},{9,13},{10,... | collective-permute-start | bytes 98312 | tf_op jit(solution)/shard_map/ppermute | solution.py:422
  8.9 2.5 %collective-permute-start.2 = (bf16[32,128]{1,0:T(8,128)(2,1)S(1)}, bf16[32,128]{1,0:T(8,128)(2,1)S(1)}, u32[]{:S(2)}, u32[]{:S(2)}) collective-permute-start(bf16[32,128]{1,0:T(8,128)(2,1)S(1)} %get-tuple-element.10.after), channel_id=1, source_target_pairs={{0,2},{1,3},{2,0},{3,1},{4,6},{5,7},{6,4},{7,5},{8,10},{9,11},{10,... | collective-permute-start | bytes 24584 | tf_op jit(solution)/shard_map/ppermute | solution.py:422
  10.1 3.1 %collective-permute-start.3 = (bf16[32,128]{1,0:T(8,128)(2,1)S(1)}, bf16[32,128]{1,0:T(8,128)(2,1)S(1)}, u32[]{:S(2)}, u32[]{:S(2)}) collective-permute-start(bf16[32,128]{1,0:T(8,128)(2,1)S(1)} %get-tuple-element.10.after), channel_id=1, source_target_pairs={{0,3},{1,7},{2,1},{3,5},{4,0},{5,11},{6,2},{7,9},{8,4},{9,15},{10,... | collective-permute-start | bytes 24584 | tf_op jit(solution)/shard_map/ppermute | solution.py:422
  13.2 1.2 %collective-permute-start.4 = (bf16[192,128]{1,0:T(8,128)(2,1)S(1)}, bf16[192,128]{1,0:T(8,128)(2,1)S(1)}, u32[]{:S(2)}, u32[]{:S(2)}) collective-permute-start(bf16[192,128]{1,0:T(8,128)(2,1)S(1)} %constant_dynamic-update-slice_fusion.prev), channel_id=1, source_target_pairs={{0,1},{1,0},{2,3},{3,2},{4,5},{5,4},{6,7},{7,6},{8,9},{9,8},{10,11... | collective-permute-start | bytes 147464 | tf_op jit(solution)/shard_map/ppermute | solution.py:422
